TPU v7x, 32 devices: a whole 2x2x4 slice. The times are simulated.
32 devices in a mesh: dp: 2 (over y), fsdp: 16 (over z, x, core).
Axes of the slice: x: 2, y: 2, z: 4, core: 2. Of those that a mesh axis runs over, the one named last changes fastest.
Arguments:
- tokens: bfloat16 [65536, 768], P(('dp', 'fsdp')), may hold values from -12 to 12
- cotangent: bfloat16 [65536, 768], P(('dp', 'fsdp')), may hold values from -12 to 12
- segment_ids: int32 [65536], P(('dp', 'fsdp')), may hold values from 0 to 2687, as said below
- first_gain: bfloat16 [768], P('fsdp'), may hold values from 0.25 to 1.75
- first_shift: bfloat16 [768], P('fsdp'), may hold values from -1.75 to 1.75
- triple_weight: bfloat16 [768, 2304], P('fsdp'), may hold values from -0.3125 to 0.3125
- query_bias: bfloat16 [768], P('fsdp'), may hold values from -3 to 3
- value_bias: bfloat16 [768], P('fsdp'), may hold values from -1.75 to 1.75
- out_weight: bfloat16 [768, 768], P('fsdp'), may hold values from -0.875 to 0.875
- out_bias: bfloat16 [768], P('fsdp'), may hold values from -1.75 to 1.75
- second_gain: bfloat16 [768], P('fsdp'), may hold values from 0.25 to 1.75
- second_shift: bfloat16 [768], P('fsdp'), may hold values from -1.75 to 1.75
- up_weight: bfloat16 [768, 3072], P('fsdp'), may hold values from -0.21875 to 0.21875
- up_bias: bfloat16 [3072], P('fsdp'), may hold values from -3 to 3
- down_weight: bfloat16 [3072, 768], P('fsdp'), may hold values from -0.109375 to 0.109375
- down_bias: bfloat16 [768], P('fsdp'), may hold values from -1.75 to 1.75
Outputs:
- block_output: bfloat16 [65536, 768], P(('dp', 'fsdp'))
- tokens_gradient: bfloat16 [65536, 768], P(('dp', 'fsdp'))
- first_gain_gradient: float32 [768], P('fsdp')
- first_shift_gradient: float32 [768], P('fsdp')
- triple_weight_gradient: float32 [768, 2304], P('fsdp')
- query_bias_gradient: float32 [768], P('fsdp')
- value_bias_gradient: float32 [768], P('fsdp')
- out_weight_gradient: float32 [768, 768], P('fsdp')
- out_bias_gradient: float32 [768], P('fsdp')
- second_gain_gradient: float32 [768], P('fsdp')
- second_shift_gradient: float32 [768], P('fsdp')
- up_weight_gradient: float32 [768, 3072], P('fsdp')
- up_bias_gradient: float32 [3072], P('fsdp')
- down_weight_gradient: float32 [3072, 768], P('fsdp')
- down_bias_gradient: float32 [768], P('fsdp')
Inputs may be any that keep to these rules, and one draw needn't show every extreme that they name: `segment_ids`: segment numbers never fall along the patches and no image spans two aligned blocks of 1024 patches; each image has 900 patches and begins its block, or has 1 to 64 patches; the first block begins with an image of 900 patches; the last patch carries exactly the largest number, 65536 // 1024 * (1024 // max(1, 25) + 2) - 1.
All inputs are finite; a program needn't handle non-finite values.
Results may differ from a plain program's by a relative error of at most 0.014.
Values may be sent and summed in bfloat16 or wider, within the bound.
A program may use at most 384 MiB of HBM per device.

v0:
```python
import functools

import jax
import jax.numpy as jnp
from jax import lax
from jax.experimental import pallas as pl
from jax.experimental.pallas import tpu as pltpu
from jax.sharding import PartitionSpec as P

H = 12
HD = 64
ROWS = 1024
EPS = 1e-06
F32 = jnp.float32
BF16 = jnp.bfloat16
VMEM_LIMIT = 60 * 1024 * 1024

ROOT_HALF = 0.7071067811865476
ROOT_INV_TWO_PI = 0.3989422804014327

NN = (((1,), (0,)), ((), ()))
NT = (((1,), (1,)), ((), ()))


def mm(a, b, dims=NN):
    return lax.dot_general(a, b, dims, preferred_element_type=F32)


def params(**kw):
    return pltpu.CompilerParams(vmem_limit_bytes=VMEM_LIMIT, **kw)


def norm_stats(x):
    mean = jnp.mean(x, axis=-1, keepdims=True)
    cen = x - mean
    var = jnp.mean(cen * cen, axis=-1, keepdims=True)
    inv = lax.rsqrt(var + EPS)
    return cen * inv, inv


MESH = pl.DeviceIdType.MESH
ANY = pl.BlockSpec(memory_space=pl.ANY)


def whereabouts():
    y = lax.axis_index("dp")
    f = lax.axis_index("fsdp")
    return y, f // 4, (f // 2) % 2, f % 2


def spot(z, x, c):
    return z * 4 + x * 2 + c


def greet(signal=True, wait=True):
    y, z, x, c = whereabouts()
    barrier = pltpu.get_barrier_semaphore()
    peers = [(1 - y, spot(z, x, c)), (y, spot(z, 1 - x, c)), (y, spot(z, x, 1 - c))]
    peers += [(y, spot((z + d) % 4, x, c)) for d in (1, 2, 3)]
    if signal:
        for peer in peers:
            pl.semaphore_signal(barrier, inc=1, device_id=peer, device_id_type=MESH)
    if wait:
        pl.semaphore_wait(barrier, len(peers))


class Mover:
    def __init__(self, send, recv, local, per):
        self.send, self.recv, self.local, self.per = send, recv, local, per
        self.y, self.z, self.x, self.c = whereabouts()

    def wide(self, r, split, y):
        return pl.ds(pl.multiple_of(y * (r // 3), 8), 2 * (r // 3)) if split else pl.ds(0, r)

    def thin(self, r, y):
        return pl.ds(pl.multiple_of(y * 2 * (r // 3), 8), r // 3)

    def copy(self, u, slot, src, dst, z=None, x=None, c=None, y=None):
        i = u * self.per + slot
        pick = lambda v, own: own if v is None else v
        peer = (pick(y, self.y), spot(pick(z, self.z), pick(x, self.x), pick(c, self.c)))
        return pltpu.make_async_remote_copy(
            src_ref=src, dst_ref=dst, send_sem=self.send.at[i], recv_sem=self.recv.at[i],
            device_id=peer, device_id_type=MESH,
        )


class Gather(Mover):
    def __init__(self, units, send, recv, local):
        super().__init__(send, recv, local, 6)
        self.units = units

    def mine(self, u):
        src, _, _, col, n, split = self.units[u]
        return src.at[self.wide(src.shape[0], split, self.y), pl.ds(col, n)]

    def held(self, u):
        src, _, hold, col, n, split = self.units[u]
        return hold.at[self.wide(src.shape[0], split, self.y), pl.ds(col, n)]

    def part(self, u, z, x, c, rows):
        _, dst, _, col, n, _ = self.units[u]
        every = slice(None)
        pick = lambda v: every if v is None else v
        return dst.at[pick(z), pick(x), pick(c), rows, pl.ds(col, n)]

    def broad(self, u):
        src, _, _, _, _, split = self.units[u]
        return self.wide(src.shape[0], split, self.y)

    def load(self, u):
        return pltpu.make_async_copy(self.mine(u), self.held(u), self.local.at[2 * u])

    def store(self, u):
        dst = self.part(u, self.z, self.x, self.c, self.broad(u))
        return pltpu.make_async_copy(self.held(u), dst, self.local.at[2 * u + 1])

    def along_z(self, u, d, out=True):
        here, there = (self.z + 4 - d) % 4, (self.z + d) % 4
        dst = self.part(u, self.z if out else here, self.x, self.c, self.broad(u))
        return self.copy(u, d - 1, self.mine(u), dst, z=there)

    def along_x(self, u, out=True):
        src = self.part(u, None, self.x, self.c, self.broad(u))
        dst = src if out else self.part(u, None, 1 - self.x, self.c, self.broad(u))
        return self.copy(u, 3, src, dst, x=1 - self.x)

    def along_y(self, u, out=True):
        r = self.units[u][0].shape[0]
        src = self.part(u, None, None, self.c, self.thin(r, self.y))
        dst = src if out else self.part(u, None, None, self.c, self.thin(r, 1 - self.y))
        return self.copy(u, 4, src, dst, y=1 - self.y)

    def along_c(self, u, out=True):
        every = pl.ds(0, self.units[u][0].shape[0])
        src = self.part(u, None, None, self.c, every)
        dst = src if out else self.part(u, None, None, 1 - self.c, every)
        return self.copy(u, 5, src, dst, c=1 - self.c)

    def stage(self, s, u):
        split = self.units[u][5]
        if s == 0:
            for d in (1, 2, 3):
                self.along_z(u, d).start()
            self.load(u).start()
        if s == 1:
            self.load(u).wait()
            self.store(u).start()
        if s == 2:
            self.store(u).wait()
            for d in (1, 2, 3):
                self.along_z(u, d, False).wait_recv()
            self.along_x(u).start()
        if s == 3:
            self.along_x(u, False).wait_recv()
            if split:
                self.along_y(u).start()
            else:
                self.along_c(u).start()
        if s == 4 and split:
            self.along_y(u, False).wait_recv()
            self.along_c(u).start()
        if s == 5:
            self.along_c(u, False).wait_recv()
            for d in (1, 2, 3):
                self.along_z(u, d).wait_send()
            self.along_x(u).wait_send()
            if split:
                self.along_y(u).wait_send()
            self.along_c(u).wait_send()


def gather_sems(units):
    return [
        pltpu.SemaphoreType.DMA((units * 6,)),
        pltpu.SemaphoreType.DMA((units * 6,)),
        pltpu.SemaphoreType.DMA((2 * units,)),
    ]


def whole(shard):
    return jax.ShapeDtypeStruct((4, 2, 2, *shard.shape), shard.dtype)


class Reduce(Mover):
    def __init__(self, units, send, recv, local):
        super().__init__(send, recv, local, 7)
        self.units = units

    def size(self, u):
        return self.units[u][0].shape[3]

    def partial(self, u, c):
        src, _, (col, _), n, _, _ = self.units[u]
        return src.at[:, :, c, :, pl.ds(col, n)]

    def load(self, u):
        return pltpu.make_async_copy(self.partial(u, self.c), self.units[u][5][0], self.local.at[u])

    def over_c(self, u):
        return self.copy(u, 0, self.partial(u, 1 - self.c), self.units[u][5][1], c=1 - self.c)

    def over_y(self, u):
        own, from_y = self.units[u][5][0], self.units[u][5][5]
        return self.copy(u, 1, own.at[:, :, self.thin(self.size(u), 1 - self.y), :], from_y, y=1 - self.y)

    def over_x(self, u):
        own, from_x = self.units[u][5][0], self.units[u][5][2]
        rows = self.wide(self.size(u), self.units[u][4], self.y)
        return self.copy(u, 2, own.at[:, 1 - self.x, rows, :], from_x, x=1 - self.x)

    def over_z(self, u, d):
        own, from_z = self.units[u][5][0], self.units[u][5][3]
        rows = self.wide(self.size(u), self.units[u][4], self.y)
        to = (self.z + d) % 4
        return self.copy(u, 2 + d, own.at[to, self.x, rows, :], from_z.at[d - 1], z=to)

    def over_last(self, u):
        last = self.units[u][5][4]
        return self.copy(u, 6, last.at[0], last.at[1], y=1 - self.y)

    def stage(self, s, u):
        _, out, (_, col), n, split, (own, from_c, from_x, from_z, last, *rest) = self.units[u]
        y, z, x = self.y, self.z, self.x
        r = self.size(u)
        rows = self.wide(r, split, y)
        if s == 0:
            self.over_c(u).start()
            self.load(u).start()
        if s == 1:
            self.load(u).wait()
            self.over_c(u).wait_recv()
            own[...] = own[...] + from_c[...]
            if split:
                self.over_y(u).start()
        if s == 2:
            if split:
                self.over_y(u).wait_recv()
                mine = self.thin(r, y)
                own[:, :, mine, :] = own[:, :, mine, :] + rest[0][...]
            self.over_x(u).start()
        if s == 3:
            self.over_x(u).wait_recv()
            for k in range(4):
                own[k, x, rows, :] = own[k, x, rows, :] + from_x[k]
            for d in (1, 2, 3):
                self.over_z(u, d).start()
        if s == 4:
            total = own[z, x, rows, :].astype(F32)
            for d in (1, 2, 3):
                self.over_z(u, d).wait_recv()
                total = total + from_z[d - 1].astype(F32)
            last[0] = total.astype(last.dtype)
            self.over_last(u).start()
        if s == 5:
            self.over_last(u).wait_recv()
            cols = pl.ds(col, n)
            if split:
                t = r // 3
                at = lambda k: pl.ds(pl.multiple_of(k * t, 8), t)
                put = lambda k, v: out.__setitem__((at(k), cols), v.astype(F32))
                put(1, last[0, at(1 - y), :].astype(F32) + last[1, at(y), :].astype(F32))
                put(2 * y, last[0, at(y), :])
                put(2 * (1 - y), last[1, at(1 - y), :])
            else:
                out[:, cols] = last[0].astype(F32) + last[1].astype(F32)
        if s == 6:
            self.over_c(u).wait_send()
            if split:
                self.over_y(u).wait_send()
            self.over_x(u).wait_send()
            for d in (1, 2, 3):
                self.over_z(u, d).wait_send()
            self.over_last(u).wait_send()


def reduce_buffers(r, n, dtype, split):
    wide = 2 * r // 3 if split else r
    shapes = [(4, 2, r, n), (4, 2, r, n), (4, wide, n), (3, wide, n), (2, wide, n)]
    if split:
        shapes.append((4, 2, r // 3, n))
    return [pltpu.VMEM(shape, dtype) for shape in shapes]


def reduce_scratch(plan):
    flat = []
    for p in plan:
        flat += reduce_buffers(*p)
    units = len(plan)
    return flat + [
        pltpu.SemaphoreType.DMA((units * 7,)),
        pltpu.SemaphoreType.DMA((units * 7,)),
        pltpu.SemaphoreType.DMA((units,)),
    ]


def reduce_work(plan, places, scratch):
    units = []
    at = 0
    for (_, n, _, split), (src, out, col) in zip(plan, places):
        count = 6 if split else 5
        units.append((src, out, col, n, split, scratch[at : at + count]))
        at += count
    return Reduce(units, *scratch[at:])


def at_hook(hook, moves, work, newest=False):
    for u, hooks in list(enumerate(moves))[:: -1 if newest else 1]:
        for s, when in enumerate(hooks):
            if when == hook:
                work.stage(s, u)


def hooked(step, per_step, which, steps, moves, work, late=False):
    if late and which == 0:

        @pl.when(step == 0)
        def _():
            greet(wait=False)

    for k in range(steps):
        if any(k * per_step + which in hooks for hooks in moves):

            @pl.when(step == k)
            def _():
                if which == 0 and k == late:
                    greet(signal=not late)
                at_hook(k * per_step + which, moves, work)


def unpack(vec_ref, ub_ref, tall_ref):
    d = vec_ref.shape[1] // 16
    f = ub_ref.shape[1] // 16
    for i in range(16):
        tile = tall_ref[i // 4, (i // 2) % 2, i % 2].astype(F32)
        vec_ref[:, i * d : (i + 1) * d] = tile[0:8, 0:d]
        ub_ref[:, i * f : i * f + 128] = tile[8:9, 0:128]
        ub_ref[:, i * f + 128 : (i + 1) * f] = tile[9:10, 0 : f - 128]


PIECES = ((0, 512), (512, 256))
FIRST_LAGS = (0, 1, 2, 4, 6, 8)


def first_body(*refs):
    vectors = refs[:9]
    t_ref, x_hbm, g_hbm = refs[9:12]
    w_hbm, vec_ref, ub_ref, qkv_hbm, ht_hbm, gt_hbm = refs[12:18]
    row_ref, tile_ref, tall_ref, vh_ref, w_ref, th_ref, x_ref, g_ref, h_ref, ht_ref, gt_ref, out_ref = refs[18:30]
    move_sem, out_sem, w_sem, *sems = refs[30:]
    rows, d = x_ref.shape
    columns = [(j, j * d + col, n) for j in range(3) for col, n in PIECES]
    units = [(tile_ref, tall_ref, vh_ref, 0, 128, False)]
    units += [(t_ref, w_ref, th_ref, col, n, True) for _, col, n in columns]
    work = Gather(units, *sems)
    moves = [[0, 1, 2, 3, 4, 5]] + [[u + lag for lag in FIRST_LAGS] for u in range(len(columns))]
    local = lambda i, src, dst: pltpu.make_async_copy(src, dst, move_sem.at[i])
    get_x, get_g = local(0, x_hbm, x_ref), local(1, g_hbm, g_ref)
    put_h, put_g = local(2, ht_ref, ht_hbm), local(3, gt_ref, gt_hbm)

    greet(wait=False)
    get_g.start()
    get_x.start()
    for i, ref in enumerate(vectors[:8]):
        row_ref[i : i + 1, 0 : ref.shape[0]] = ref[...].astype(F32).reshape(1, -1)
    up = vectors[8][...].astype(F32).reshape(1, -1)
    row_ref[8:9, :] = up[:, :128]
    row_ref[9:10, 0 : up.shape[1] - 128] = up[:, 128:]
    tile_ref[...] = row_ref[...].astype(BF16)
    greet(signal=False)
    at_hook(0, moves, work)
    get_g.wait()
    for t in range(4):
        part = slice(t * (rows // 4), (t + 1) * (rows // 4))
        gt_ref[:, part] = g_ref[part, :].T
        at_hook(1 + t, moves, work)
    put_g.start()
    get_x.wait()
    at_hook(5, moves, work)
    unpack(vec_ref, ub_ref, tall_ref)
    for t in range(4):
        part = slice(t * (rows // 4), (t + 1) * (rows // 4))
        n, _ = norm_stats(x_ref[part, :].astype(F32))
        h = (n * vec_ref[0:1, :] + vec_ref[1:2, :]).astype(BF16)
        h_ref[part, :] = h
        ht_ref[:, part] = h.T
        at_hook(6 + t, moves, work)
    put_h.start()

    def place(u):
        _, col, n = columns[u]
        return pltpu.make_async_copy(out_ref.at[u % 2, :, pl.ds(0, n)], qkv_hbm.at[:, pl.ds(col, n)], out_sem.at[u])

    def keep(u):
        _, col, n = columns[u]
        cols = pl.ds(col, n)
        return pltpu.make_async_copy(w_ref.at[:, :, :, :, cols], w_hbm.at[:, :, :, :, cols], w_sem.at[u])

    for u, (j, col, n) in enumerate(columns):
        if u:
            at_hook(9 + u, moves, work)
        keep(u).start()
        if u >= 2:
            place(u - 2).wait()
        own = slice(col - j * d, col - j * d + n)

        @pl.loop(0, 4)
        def _(t):
            part = pl.ds(pl.multiple_of(t * (rows // 4), 8), rows // 4)
            p = mm(h_ref[part, :], w_ref[:, :, :, :, col : col + n].reshape(d, n))
            if j == 0:
                p = (p + vec_ref[2:3, own]) * 0.125
            if j == 2:
                p = p + vec_ref[3:4, own]
            out_ref[u % 2, part, 0:n] = p.astype(BF16)

        place(u).start()
    put_g.wait()
    put_h.wait()
    for u in range(len(columns)):
        keep(u).wait()
        if u >= len(columns) - 2:
            place(u).wait()


def first(vectors, triple, x, g):
    rows, d = x.shape
    vmem = pl.BlockSpec(memory_space=pltpu.VMEM)
    across = pltpu.VMEM((d, rows), BF16)
    down = pltpu.VMEM((rows, d), BF16)
    pieces = 3 * len(PIECES)
    return pl.pallas_call(
        first_body,
        in_specs=[vmem] * 9 + [ANY] * 3,
        out_specs=[ANY, vmem, vmem, ANY, ANY, ANY],
        out_shape=[
            whole(triple),
            jax.ShapeDtypeStruct((8, d), F32),
            jax.ShapeDtypeStruct((1, 4 * d), F32),
            jax.ShapeDtypeStruct((rows, 3 * d), BF16),
            jax.ShapeDtypeStruct((d, rows), BF16),
            jax.ShapeDtypeStruct((d, rows), BF16),
        ],
        scratch_shapes=[
            pltpu.VMEM((16, 128), F32),
            pltpu.VMEM((16, 128), BF16),
            pltpu.VMEM((4, 2, 2, 16, 128), BF16),
            pltpu.VMEM((16, 128), BF16),
            pltpu.VMEM((4, 2, 2, *triple.shape), BF16),
            pltpu.VMEM(triple.shape, BF16),
            down,
            down,
            down,
            across,
            across,
            pltpu.VMEM((2, rows, PIECES[0][1]), BF16),
            pltpu.SemaphoreType.DMA((4,)),
            pltpu.SemaphoreType.DMA((pieces,)),
            pltpu.SemaphoreType.DMA((pieces,)),
            *gather_sems(1 + pieces),
        ],
        compiler_params=params(collective_id=0, has_side_effects=True),
        name="first",
    )(*vectors, triple, x, g)


def proj_body(x_ref, vec_ref, w_ref, qkv_ref, ht_ref):
    d = x_ref.shape[1]
    n, _ = norm_stats(x_ref[...].astype(F32))
    h = (n * vec_ref[0:1, :] + vec_ref[1:2, :]).astype(BF16)
    ht_ref[...] = h.T
    for j in range(3):
        cols = pl.ds(j * d, d)
        p = mm(h, w_ref[:, cols])
        if j == 0:
            p = (p + vec_ref[2:3, :]) * 0.125
        if j == 2:
            p = p + vec_ref[3:4, :]
        qkv_ref[:, cols] = p.astype(BF16)


def project(x, vec, w):
    rows, d = x.shape
    cols = w.shape[1]
    tile = 512
    return pl.pallas_call(
        proj_body,
        grid=(rows // tile,),
        in_specs=[
            pl.BlockSpec((tile, d), lambda i: (i, 0)),
            pl.BlockSpec((8, d), lambda i: (0, 0)),
            pl.BlockSpec((d, cols), lambda i: (0, 0)),
        ],
        out_specs=[
            pl.BlockSpec((tile, cols), lambda i: (i, 0)),
            pl.BlockSpec((d, tile), lambda i: (0, i)),
        ],
        out_shape=[jax.ShapeDtypeStruct((rows, cols), BF16), jax.ShapeDtypeStruct((d, rows), BF16)],
        compiler_params=params(),
        name="project",
        cost_estimate=pl.CostEstimate(
            flops=2 * rows * d * cols, bytes_accessed=2 * rows * (d + cols), transcendentals=0
        ),
    )(x, vec, w)


QT = 256
GATHER_CUT = 6
REDUCE_CUT = 3
GATHER_LAGS = (0, 1, 3, 5, 7, 9)
REDUCE_LAGS = (0, 1, 4, 7, 10, 12, 12)


LOG2E = 1.4426950408889634


def swap(value):
    return jnp.concatenate([value[:, HD:], value[:, :HD]], axis=1)


def twice(value, own):
    return jnp.where(own, value, swap(value))


def unit_list(widths, cut):
    units = [(0, 0, widths[0])]
    for i, w in enumerate(widths[1:]):
        units += [(i + 1, j * (w // cut), w // cut) for j in range(cut)]
    return units


def attend_body(hosting, *refs):
    q_ref, k_ref, v_ref, seg_ref = refs[:4]
    if hosting:
        shards = refs[4:7]
        o_ref, p_ref, inv_ref = refs[7:10]
        full = refs[10:13]
        bias_ref, pair_ref = refs[13:15]
        hold = refs[15:18]
        units = [(shards[i], full[i], hold[i], col, n, True) for i, col, n in unit_list([s.shape[1] for s in shards], GATHER_CUT)]
        work = Gather(units, *refs[18:])
        moves = [[2 + u + lag for lag in GATHER_LAGS] for u in range(len(units))]
    else:
        o_ref, p_ref, inv_ref, bias_ref, pair_ref = refs[4:]
    step = pl.program_id(0) * pl.num_programs(1) + pl.program_id(1)
    rows = q_ref.shape[0]

    @pl.when(pl.program_id(1) == 0)
    def _():
        seg = seg_ref[...].astype(F32)
        column = jnp.broadcast_to(seg, (8, rows)).T[:, 0:1]
        bias_ref[...] = jnp.where(column == seg, 0.0, -1e30)

    lower = lax.broadcasted_iota(jnp.int32, (1, 128), 1) < HD
    lower = lax.broadcasted_iota(jnp.int32, (1, 128), 1) < HD
    lower = lax.broadcasted_iota(jnp.int32, (1, 128), 1) < HD
    sums = []
    for hh in range(2):
        if hosting:
            hooked(step, 2, hh, 12, moves, work, True)
        own = lower if hh == 0 else ~lower
        q = q_ref[...].astype(F32) * LOG2E
        high = q.astype(BF16)
        low = (q - high.astype(F32)).astype(BF16)
        pair_ref[0, hh] = jnp.where(own, high, swap(low))
        pair_ref[1, hh] = twice(k_ref[...], own)
        pair_ref[2, hh] = jnp.where(own, v_ref[...], jnp.ones_like(v_ref[...]))
        if hh == 1:
            sums.append(mm(p_ref[0], pair_ref[2, 0]))
        for t in range(rows // QT):
            sl = pl.ds(t * QT, QT)
            s = mm(pair_ref[0, hh, sl, :], pair_ref[1, hh], NT) + bias_ref[sl, :]
            p_ref[hh, sl, :] = jnp.exp2(s - jnp.max(s, axis=-1, keepdims=True)).astype(BF16)
    sums.append(mm(p_ref[1], pair_ref[2, 1]))
    inv = 1.0 / swap(jnp.where(lower, sums[1], sums[0]))
    inv_ref[...] = inv
    o_ref[...] = (jnp.where(lower, sums[0], sums[1]) * inv).astype(BF16)


def attend(qkv, segr, shards=()):
    rows = qkv.shape[0]
    d = qkv.shape[1] // 3
    mb = rows // ROWS
    pairs = d // 128
    extra = dict(collective_id=1, has_side_effects=True) if shards else {}
    return pl.pallas_call(
        functools.partial(attend_body, bool(shards)),
        grid=(mb, pairs),
        in_specs=[
            pl.BlockSpec((ROWS, 128), lambda m, h: (m, h)),
            pl.BlockSpec((ROWS, 128), lambda m, h: (m, pairs + h)),
            pl.BlockSpec((ROWS, 128), lambda m, h: (m, 2 * pairs + h)),
            pl.BlockSpec((None, 1, ROWS), lambda m, h: (m, 0, 0)),
            *[ANY for _ in shards],
        ],
        out_specs=[
            pl.BlockSpec((ROWS, 128), lambda m, h: (m, h)),
            pl.BlockSpec((None, 2, ROWS, ROWS), lambda m, h: (m, h, 0, 0)),
            pl.BlockSpec((ROWS, 128), lambda m, h: (m, h)),
            *[ANY for _ in shards],
        ],
        out_shape=[
            jax.ShapeDtypeStruct((rows, d), BF16),
            jax.ShapeDtypeStruct((mb, 2 * pairs, ROWS, ROWS), BF16),
            jax.ShapeDtypeStruct((rows, d), F32),
            *[whole(s) for s in shards],
        ],
        scratch_shapes=[pltpu.VMEM((ROWS, ROWS), F32), pltpu.VMEM((3, 2, ROWS, 128), BF16)]
        + ([pltpu.VMEM(s.shape, s.dtype) for s in shards] + gather_sems(1 + 2 * GATHER_CUT) if shards else []),
        compiler_params=params(**extra),
        name="attend",
        cost_estimate=pl.CostEstimate(
            flops=mb * pairs * 2 * 4 * ROWS * ROWS * 256,
            bytes_accessed=mb * pairs * 2 * ROWS * ROWS * 2,
            transcendentals=mb * pairs * 2 * ROWS * ROWS,
        ),
    )(qkv, qkv, qkv, segr, *shards)


def attend_back_body(plan, *refs):
    q_ref, k_ref, v_ref, p_ref, o_ref, g_ref, inv_ref = refs[:7]
    hosting = plan is not None
    if hosting:
        parts = refs[7:10]
        d_ref = refs[10]
        results = refs[11:14]
        ds_ref = refs[14]
        places = [(parts[i], results[i], (col, col)) for i, col, _ in unit_list([p.shape[4] for p in parts], REDUCE_CUT)]
        work = reduce_work(plan, places, refs[15:])
        moves = [[max(0, 2 * u - 1) + lag for lag in REDUCE_LAGS] for u in range(len(places))]
    else:
        d_ref, ds_ref = refs[7:]
    step = pl.program_id(0) * pl.num_programs(1) + pl.program_id(1)
    rows = q_ref.shape[0]
    lower = lax.broadcasted_iota(jnp.int32, (1, 128), 1) < HD
    dk_parts = []
    dv_parts = []
    dq_parts = []
    for hh in range(2):
        if hosting:
            hooked(step, 2, hh, 12, moves, work)
        own = lower if hh == 0 else ~lower
        half = slice(hh * HD, (hh + 1) * HD)
        g = g_ref[...].astype(F32) * inv_ref[...]
        high = g.astype(BF16)
        low = (g - high.astype(F32)).astype(BF16)
        pair = jnp.where(own, high, swap(low))
        center = jnp.sum(jnp.where(own, g * o_ref[...].astype(F32), 0.0), axis=-1, keepdims=True)
        v = twice(v_ref[...], own)
        for t in range(rows // QT):
            sl = pl.ds(t * QT, QT)
            ts = slice(t * QT, (t + 1) * QT)
            d_soft = mm(pair[ts, :], v, NT)
            ds_ref[hh, sl, :] = (p_ref[hh, sl, :].astype(F32) * (d_soft - center[ts, :])).astype(BF16)
        dv = mm(pair.T, p_ref[hh])
        dv_parts.append(dv[:HD, :] + dv[HD:, :])
        dk_parts.append(mm(q_ref[...].T[half, :], ds_ref[hh]))
        dq_parts.append(mm(ds_ref[hh], k_ref[...]))
    d_ref[0] = (jnp.where(lower, dq_parts[0], dq_parts[1]) * 0.125).astype(BF16)
    d_ref[1] = jnp.concatenate(dk_parts, axis=0).T.astype(BF16)
    d_ref[2] = jnp.concatenate(dv_parts, axis=0).T.astype(BF16)


def attend_back(qkv, soft, mixed, d_mixed, inv, grads=()):
    rows = qkv.shape[0]
    d = qkv.shape[1] // 3
    mb = rows // ROWS
    pairs = d // 128
    blk = pl.BlockSpec((ROWS, 128), lambda m, h: (m, h))
    plan = None
    results = []
    extra = {}
    grads = [g.reshape(4, 2, 2, g.shape[0] // 16, g.shape[1]) for g in grads]
    if grads:
        plan = [(grads[i].shape[3], n, BF16, True) for i, _, n in unit_list([g.shape[4] for g in grads], REDUCE_CUT)]
        results = [jax.ShapeDtypeStruct(g.shape[3:], F32) for g in grads]
        extra = dict(collective_id=2, has_side_effects=True)
    return pl.pallas_call(
        functools.partial(attend_back_body, plan),
        grid=(mb, pairs),
        in_specs=[
            blk,
            pl.BlockSpec((ROWS, 128), lambda m, h: (m, pairs + h)),
            pl.BlockSpec((ROWS, 128), lambda m, h: (m, 2 * pairs + h)),
            pl.BlockSpec((None, 2, ROWS, ROWS), lambda m, h: (m, h, 0, 0)),
            blk,
            blk,
            blk,
            *[ANY for _ in grads],
        ],
        out_specs=[
            pl.BlockSpec((3, ROWS, 128), lambda m, h: (0, m, h)),
            *[pl.BlockSpec(r.shape, lambda m, h: (0, 0)) for r in results],
        ],
        out_shape=[jax.ShapeDtypeStruct((3, rows, d), BF16), *results],
        scratch_shapes=[pltpu.VMEM((2, ROWS, ROWS), BF16)] + (reduce_scratch(plan) if grads else []),
        compiler_params=params(**extra),
        name="attend_back",
        cost_estimate=pl.CostEstimate(
            flops=mb * pairs * 2 * 8 * ROWS * ROWS * 256,
            bytes_accessed=mb * pairs * 2 * ROWS * ROWS * 2,
            transcendentals=0,
        ),
    )(qkv, qkv, qkv, soft, mixed, d_mixed, inv, *grads)


def out_body(x_ref, m_ref, w_ref, vec_ref, resid_ref, h_ref, ht_ref):
    resid = x_ref[...].astype(F32) + mm(m_ref[...], w_ref[...]) + vec_ref[4:5, :]
    resid_ref[...] = resid
    n, _ = norm_stats(resid)
    h = (n * vec_ref[5:6, :] + vec_ref[6:7, :]).astype(BF16)
    h_ref[...] = h
    ht_ref[...] = h.T


def out_project(x, mixed, w, vec):
    rows, d = x.shape
    tile = 512
    blk = pl.BlockSpec((tile, d), lambda i: (i, 0))
    return pl.pallas_call(
        out_body,
        grid=(rows // tile,),
        in_specs=[blk, blk, pl.BlockSpec((d, d), lambda i: (0, 0)), pl.BlockSpec((8, d), lambda i: (0, 0))],
        out_specs=[blk, blk, pl.BlockSpec((d, tile), lambda i: (0, i))],
        out_shape=[
            jax.ShapeDtypeStruct((rows, d), F32),
            jax.ShapeDtypeStruct((rows, d), BF16),
            jax.ShapeDtypeStruct((d, rows), BF16),
        ],
        compiler_params=params(),
        name="out_project",
        cost_estimate=pl.CostEstimate(
            flops=2 * rows * d * d, bytes_accessed=rows * d * 12, transcendentals=0
        ),
    )(x, mixed, w, vec)


FC = 512
RT = 1024


def gelu_parts(u):
    cdf = 0.5 * (1.0 + lax.erf(u * ROOT_HALF))
    bell = jnp.exp(-0.5 * u * u) * ROOT_INV_TWO_PI
    return u * cdf, cdf + u * bell


def mlp_body(h_ref, ht_ref, g_ref, gt_ref, wu_ref, bu_ref, wd_ref, acc_ref, dh_ref, dwu_ref, dwd_ref, dbu_ref,
             act_ref, du_ref):
    rows = h_ref.shape[0]

    @pl.when(pl.program_id(0) == 0)
    def _():
        acc_ref[...] = jnp.zeros_like(acc_ref)
        dh_ref[...] = jnp.zeros_like(dh_ref)

    wu = wu_ref[...]
    wd = wd_ref[...]
    dbu_ref[...] = jnp.zeros_like(dbu_ref)

    @pl.loop(0, rows // RT)
    def _(t):
        sl = pl.ds(pl.multiple_of(t * RT, RT), RT)
        u = mm(h_ref[sl, :], wu) + bu_ref[...]
        act, slope = gelu_parts(u)
        act_ref[sl, :] = act.astype(BF16)
        du = mm(g_ref[sl, :], wd, NT) * slope
        dbu_ref[...] += jnp.sum(du, axis=0, keepdims=True)
        du_ref[sl, :] = du.astype(BF16)
        acc_ref[sl, :] += mm(act_ref[sl, :], wd)
        dh_ref[sl, :] += mm(du_ref[sl, :], wu, NT)

    dwu_ref[...] = mm(ht_ref[...], du_ref[...]).astype(dwu_ref.dtype)
    dwd_ref[...] = mm(gt_ref[...], act_ref[...]).T.astype(dwd_ref.dtype)


def mlp(h, ht, g, gt, wu, bu, wd):
    rows, d = h.shape
    ff = wu.shape[1]
    one = pl.Buffered(1)
    whole = pl.BlockSpec((rows, d), lambda c: (0, 0), pipeline_mode=one)
    whole_t = pl.BlockSpec((d, rows), lambda c: (0, 0), pipeline_mode=one)
    return pl.pallas_call(
        mlp_body,
        grid=(ff // FC,),
        in_specs=[
            whole,
            whole_t,
            whole,
            whole_t,
            pl.BlockSpec((d, FC), lambda c: (0, c)),
            pl.BlockSpec((1, FC), lambda c: (0, c)),
            pl.BlockSpec((FC, d), lambda c: (c, 0)),
        ],
        out_specs=[
            whole,
            whole,
            pl.BlockSpec((d, FC), lambda c: (0, c)),
            pl.BlockSpec((FC, d), lambda c: (c, 0)),
            pl.BlockSpec((1, FC), lambda c: (0, c)),
        ],
        out_shape=[
            jax.ShapeDtypeStruct((rows, d), F32),
            jax.ShapeDtypeStruct((rows, d), F32),
            jax.ShapeDtypeStruct((d, ff), BF16),
            jax.ShapeDtypeStruct((ff, d), BF16),
            jax.ShapeDtypeStruct((1, ff), F32),
        ],
        scratch_shapes=[pltpu.VMEM((rows, FC), BF16), pltpu.VMEM((rows, FC), BF16)],
        compiler_params=params(),
        name="mlp",
        cost_estimate=pl.CostEstimate(
            flops=12 * rows * d * ff, bytes_accessed=rows * d * 20 + 8 * d * ff, transcendentals=3 * rows * ff
        ),
    )(h, ht, g, gt, wu, bu, wd)


def fold(ref, row, step, value):
    part = jnp.sum(value, axis=0, keepdims=True)

    @pl.when(step == 0)
    def _():
        ref[row : row + 1, :] = part

    @pl.when(step != 0)
    def _():
        ref[row : row + 1, :] += part


def norm_pull(grad, n, inv, gain):
    dn = grad * gain
    plain = jnp.mean(dn, axis=-1, keepdims=True)
    cross = jnp.mean(dn * n, axis=-1, keepdims=True)
    return inv * (dn - plain - n * cross)


def mid_body(resid_ref, acc_ref, dh_ref, g_ref, mixed_ref, w_ref, vec_ref,
             y_ref, dr_ref, dm_ref, dw_ref, dvec_ref, sum_ref):
    step = pl.program_id(0)
    resid = resid_ref[...]
    y_ref[...] = (resid + acc_ref[...] + vec_ref[7:8, :]).astype(BF16)
    g = g_ref[...].astype(F32)
    n, inv = norm_stats(resid)
    dh = dh_ref[...]
    dr = g + norm_pull(dh, n, inv, vec_ref[5:6, :])
    dr_ref[...] = dr
    fold(dvec_ref, 4, step, dr)
    fold(dvec_ref, 5, step, dh * n)
    fold(dvec_ref, 6, step, dh)
    fold(dvec_ref, 7, step, g)
    low = dr.astype(BF16)
    dm_ref[...] = mm(low, w_ref[...], NT).astype(BF16)
    dw = mm(mixed_ref[...].T, low)

    @pl.when(step == 0)
    def _():
        sum_ref[...] = dw
        dvec_ref[0:4, :] = jnp.zeros((4, dvec_ref.shape[1]), F32)

    @pl.when(step != 0)
    def _():
        sum_ref[...] += dw

    @pl.when(step == pl.num_programs(0) - 1)
    def _():
        dw_ref[...] = sum_ref[...].astype(dw_ref.dtype)


def middle(resid, acc, dh, g, mixed, w, vec):
    rows, d = resid.shape
    tile = 512
    blk = pl.BlockSpec((tile, d), lambda i: (i, 0))
    mat = pl.BlockSpec((d, d), lambda i: (0, 0))
    eight = pl.BlockSpec((8, d), lambda i: (0, 0))
    return pl.pallas_call(
        mid_body,
        grid=(rows // tile,),
        in_specs=[blk, blk, blk, blk, blk, mat, eight],
        out_specs=[blk, blk, blk, mat, eight],
        out_shape=[
            jax.ShapeDtypeStruct((rows, d), BF16),
            jax.ShapeDtypeStruct((rows, d), F32),
            jax.ShapeDtypeStruct((rows, d), BF16),
            jax.ShapeDtypeStruct((d, d), BF16),
            jax.ShapeDtypeStruct((8, d), F32),
        ],
        scratch_shapes=[pltpu.VMEM((d, d), F32)],
        compiler_params=params(),
        name="middle",
        cost_estimate=pl.CostEstimate(
            flops=4 * rows * d * d, bytes_accessed=rows * d * 24, transcendentals=0
        ),
    )(resid, acc, dh, g, mixed, w, vec)


PHASES = 3
FINAL_TILE = 256


def finish_body(plan, ht_ref, part_ref, tile_ref, x_ref, dr_ref, w_hbm, vec_ref, dvec_ref, dbu_ref, dx_ref, *refs):
    step = pl.program_id(0)
    d = x_ref.shape[1]
    if plan is None:
        dw_ref, sums_ref, w_ref, w_sem = refs
    else:
        out_ref, small_ref, w_ref, w_sem, sums_ref, grad_ref, tall_ref = refs[:7]
        places = [(grad_ref.at[j], out_ref, (col, j * d + col)) for j in range(PHASES) for col, _ in PIECES]
        places.append((tall_ref, small_ref, (0, 0)))
        work = reduce_work(plan, places, refs[7:])
        vectors = len(places) - 1
        last = vectors - 1 + ht_ref.shape[1] // FINAL_TILE
        moves = FINISH_MOVES

    fetch = pltpu.make_async_copy(w_hbm, w_ref, w_sem)

    @pl.when(step == 0)
    def _():
        if plan is not None:
            greet(wait=False)
        fetch.start()
        sums_ref[...] = dvec_ref[...]

    for i, (col, n) in enumerate(PIECES):

        @pl.when(step < PHASES)
        def _():
            cols = pl.ds(col, n)
            dw = mm(ht_ref[...], part_ref[0, :, cols]).astype(BF16)
            if plan is None:
                dw_ref[:, cols] = dw
            else:
                grad_ref[step, :, :, :, :, cols] = dw.reshape(4, 2, 2, d // 16, n)

        if plan is not None:
            for j in range(PHASES):

                @pl.when(step == j)
                def _():
                    if i == 0 and j == 0:
                        greet(signal=False)
                    at_hook(2 * j + i, moves, work, True)

    for j, row in ((0, 2), (2, 3)):

        @pl.when(step == j)
        def _():
            sums_ref[row : row + 1, :] = jnp.sum(part_ref[0].astype(F32), axis=0, keepdims=True)

    @pl.when(step == PHASES)
    def _():
        fetch.wait()

    @pl.when(step >= PHASES)
    def _():
        n, inv = norm_stats(x_ref[...].astype(F32))
        dh = None
        for j in range(3):
            term = mm(tile_ref[j], w_ref[:, pl.ds(j * d, d)], NT)
            dh = term if dh is None else dh + term
        fold(sums_ref, 0, step - PHASES, dh * n)
        fold(sums_ref, 1, step - PHASES, dh)
        dx_ref[...] = (dr_ref[...] + norm_pull(dh, n, inv, vec_ref[0:1, :])).astype(BF16)

    if plan is not None:
        for k in range(2 * PHASES, last + 1):

            @pl.when(step == k - PHASES)
            def _():
                if k == last:
                    pack(tall_ref, sums_ref, dbu_ref)
                    for hook in range(last, 1 + max(max(m) for m in moves)):
                        at_hook(hook, moves, work, True)
                else:
                    at_hook(k, moves, work, True)


FINISH_MOVES = [
    [0, 1, 5, 8, 12, 14, 18],
    [1, 2, 6, 9, 12, 14, 18],
    [2, 3, 7, 10, 13, 15, 18],
    [3, 4, 8, 11, 14, 16, 18],
    [4, 5, 9, 12, 14, 16, 18],
    [5, 6, 11, 13, 15, 17, 18],
    [13, 14, 14, 15, 16, 17, 18],
]


def pack(tall_ref, sums_ref, dbu_ref):
    d = sums_ref.shape[1] // 16
    f = dbu_ref.shape[1] // 16
    for i in range(16):
        tile = tall_ref.at[i // 4, (i // 2) % 2, i % 2]
        tile[0:8, 0:d] = sums_ref[:, i * d : (i + 1) * d]
        tile[8:9, 0:128] = dbu_ref[:, i * f : i * f + 128]
        tile[9:10, 0 : f - 128] = dbu_ref[:, i * f + 128 : (i + 1) * f]


def finish(x, dr, ht, dqkv, w, vec, dvec, dbu, near):
    rows, d = x.shape
    tiles = rows // FINAL_TILE
    row = lambda s: jnp.maximum(s - PHASES, 0)
    one = pl.Buffered(1)
    eight = pl.BlockSpec((8, d), lambda s: (0, 0))
    if near:
        plan = [(d // 16, n, BF16, True) for _ in range(PHASES) for _, n in PIECES] + [(16, 128, F32, False)]
        shapes = [jax.ShapeDtypeStruct((d // 16, 3 * d), F32), jax.ShapeDtypeStruct((16, 128), F32)]
        specs = [pl.BlockSpec(s.shape, lambda s: (0, 0)) for s in shapes]
        scratch = [
            pltpu.VMEM((8, d), F32),
            pltpu.VMEM((PHASES, 4, 2, 2, d // 16, d), BF16),
            pltpu.VMEM((4, 2, 2, 16, 128), F32),
        ] + reduce_scratch(plan)
        extra = dict(collective_id=3, has_side_effects=True)
    else:
        plan = None
        shapes = [jax.ShapeDtypeStruct((d, 3 * d), BF16), jax.ShapeDtypeStruct((8, d), F32)]
        specs = [pl.BlockSpec((d, d), lambda s: (0, jnp.minimum(s, PHASES - 1))), eight]
        scratch = []
        extra = {}
    return pl.pallas_call(
        functools.partial(finish_body, plan),
        grid=(PHASES + tiles,),
        in_specs=[
            pl.BlockSpec((d, rows), lambda s: (0, 0), pipeline_mode=one),
            pl.BlockSpec((1, rows, d), lambda s: (jnp.minimum(s, PHASES - 1), 0, 0)),
            pl.BlockSpec((3, FINAL_TILE, d), lambda s: (0, row(s), 0)),
            pl.BlockSpec((FINAL_TILE, d), lambda s: (row(s), 0)),
            pl.BlockSpec((FINAL_TILE, d), lambda s: (row(s), 0)),
            ANY,
            eight,
            eight,
            pl.BlockSpec(dbu.shape, lambda s: (0, 0)),
        ],
        out_specs=[pl.BlockSpec((FINAL_TILE, d), lambda s: (row(s), 0)), *specs],
        out_shape=[jax.ShapeDtypeStruct((rows, d), BF16), *shapes],
        scratch_shapes=[pltpu.VMEM((d, 3 * d), BF16), pltpu.SemaphoreType.DMA(()), *scratch],
        compiler_params=params(**extra),
        name="finish",
        cost_estimate=pl.CostEstimate(
            flops=12 * rows * d * d, bytes_accessed=rows * d * 20, transcendentals=0
        ),
    )(ht, dqkv, dqkv, x, dr, w, vec, dvec, dbu)


def on_device(tokens, cotangent, segment_ids, *shards):
    gather = lambda s: lax.all_gather(s, "fsdp", axis=0, tiled=True)
    n = lax.axis_size("fsdp")
    near = n == 16 and lax.axis_size("dp") == 2
    triple_s, out_s, up_s, down_s = (s for s in shards if s.ndim == 2)
    rows, d = tokens.shape
    up_bias_s = shards[10]
    eights = [s for i, s in enumerate(shards) if s.ndim == 1 and i != 10]
    flat = lambda w: w.reshape(-1, w.shape[-1])
    if near:
        triple_weight, vec, up_bias, qkv, first_t, cot_t = first(eights + [up_bias_s], triple_s, tokens, cotangent)
        triple_weight = flat(triple_weight)
    else:
        triple_weight = gather(triple_s)
        packed = gather(jnp.concatenate(eights + [up_bias_s]).reshape(1, -1)).astype(F32)
        m = eights[0].shape[0]
        vec = jnp.stack([packed[:, i * m : (i + 1) * m].reshape(-1) for i in range(8)])
        up_bias = packed[:, 8 * m :].reshape(1, -1)
        qkv, first_t = project(tokens, vec, triple_weight)
        cot_t = cotangent.T

    segr = segment_ids.reshape(rows // ROWS, 1, ROWS)
    if near:
        mixed, soft, inv, *full = attend(qkv, segr, (out_s, up_s, down_s))
        out_weight, up_weight, down_weight = (flat(w) for w in full)
    else:
        mixed, soft, inv = attend(qkv, segr)
        out_weight, up_weight, down_weight = gather(out_s), gather(up_s), gather(down_s)
    resid, h, ht = out_project(tokens, mixed, out_weight, vec)
    acc, dh, dwu, dwd, dbu = mlp(h, ht, cotangent, cot_t, up_weight, up_bias, down_weight)
    y, dr, dm, dwo, dvec = middle(resid, acc, dh, cotangent, mixed, out_weight, vec)
    if near:
        dqkv, out_grad, up_grad, down_grad = attend_back(qkv, soft, mixed, dm, inv, (dwo, dwu, dwd))
        dx, triple_grad, small = finish(tokens, dr, first_t, dqkv, triple_weight, vec, dvec, dbu, True)
        m = d // n
        small_grads = [small[i, :m] for i in range(8)]
        up_bias_grad = jnp.concatenate([small[8], small[9, : up_bias_s.shape[0] - 128]])
    else:
        (dqkv,) = attend_back(qkv, soft, mixed, dm, inv)
        dx, dwt, dvec = finish(tokens, dr, first_t, dqkv, triple_weight, vec, dvec, dbu, False)
        small = jnp.concatenate([dvec[i].reshape(n, -1) for i in range(8)] + [dbu.reshape(n, -1)], axis=1)
        small = lax.psum_scatter(small, "fsdp", scatter_dimension=0, tiled=True).reshape(-1)
        small = lax.psum(small, "dp")
        total = lambda p: lax.psum(lax.psum_scatter(p, "fsdp", scatter_dimension=0, tiled=True), "dp").astype(F32)
        triple_grad, out_grad, up_grad, down_grad = total(dwt), total(dwo), total(dwu), total(dwd)
        m = d // n
        small_grads = [small[i * m : (i + 1) * m] for i in range(8)]
        up_bias_grad = small[8 * m :]
    dg1, ds1, dqb, dvb, dob, dg2, ds2, ddb = small_grads
    return (
        y, dx, dg1, ds1, triple_grad, dqb, dvb, out_grad, dob, dg2, ds2, up_grad, up_bias_grad, down_grad, ddb,
    )


def solution(mesh):
    tok = P(("dp", "fsdp"), None)
    vec = P("fsdp")
    mat = P("fsdp", None)
    weights = (vec, vec, mat, vec, vec, mat, vec, vec, vec, mat, vec, mat, vec)
    return jax.shard_map(
        on_device,
        mesh=mesh,
        in_specs=(tok, tok, P(("dp", "fsdp")), *weights),
        out_specs=(tok, tok, *weights),
        check_vma=False,
    )
```

profile of v0, /device:TPU:0, one launch (start us, length us, event | category | flops | bytes accessed | tf_op | source)
XLA Modules:
  0.0 346.4 jit_solution(17572165252253491972)
XLA Ops:
  0.6 42.1 %first.1 = (bf16[4,2,2,48,2304]{4,3,2,1,0:T(8,128)(2,1)}, f32[8,768]{1,0:T(8,128)}, f32[1,3072]{1,0:T(1,128)}, bf16[2048,2304]{1,0:T(8,128)(2,1)}, bf16[768,2048]{1,0:T(8,128)(2,1)}, /*index=5*/bf16[768,2048]{1,0:T(8,128)(2,1)}) custom-call(bf16[48]{0:T(256)(128)(2,1)} %refs_0_.1, bf16[48]{0:T(256)(128)(2,1)} %refs_1_.1, bf16[48]{0:T(256)(128)(2,1)} %refs_2_.1, ...), custom_call_target="tpu_custom_call" | custom-call | tf_op jit(solution)/shard_map/first/pallas_call | solution.py:432
  42.8 69.3 %attend.1 = (bf16[2048,768]{1,0:T(8,128)(2,1)}, bf16[2,12,1024,1024]{3,2,1,0:T(8,128)(2,1)}, f32[2048,768]{1,0:T(8,128)}, bf16[4,2,2,48,768]{4,3,2,1,0:T(8,128)(...) custom-call(bf16[2048,2304]{1,0:T(8,128)(2,1)} %get-tuple-element.47.refs_0_.refs_1_.refs_2_, ...), custom_call_target="tpu_custom_call" | custom-call | flops 25769803776 | bytes 50331648 | tf_op jit(solution)/shard_map/attend/pallas_call | solution.py:586
  112.1 9.9 %out_project.1 = (f32[2048,768]{1,0:T(8,128)}, bf16[2048,768]{1,0:T(8,128)(2,1)}, bf16[768,2048]{1,0:T(8,128)(2,1)}) custom-call(bf16[2048,768]{1,0:T(8,128)(2,1)} %x_ref.3, bf16[2048,768]{1,0:T(8,128)(2,1)} %get-tuple-element.48.m_ref.mixed_ref.refs_4_, bf16[768,768]{1,0:T(8,128)(2,1)} %bitcast.28, f32[8,768]{1,0:T(8,128)} %get-tuple-element.50.vec_ref), custom_call_target="tpu_custom_call" | custom-call | flops 2415919104 | bytes 18874368 | tf_op jit(solution)/shard_map/out_project/pallas_call | solution.py:720
  122.0 72.3 %mlp.1 = (f32[2048,768]{1,0:T(8,128)}, f32[2048,768]{1,0:T(8,128)}, bf16[768,3072]{1,0:T(8,128)(2,1)}, bf16[3072,768]{1,0:T(8,128)(2,1)}, f32[1,3072]{1,0:T(1,128)}) custom-call(bf16[2048,768]{1,0:T(8,128)(2,1)} %get-tuple-element.52.h_ref, bf16[768,2048]{1,0:T(8,128)(2,1)} %get-tuple-element.53.ht_ref, bf16[2048,768]{1,0:T(8,128)(2,1)} %g_ref.3, ...), custom_call_target="tpu_custom_call" | custom-call | flops 57982058496 | bytes 50331648 | tf_op jit(solution)/shard_map/mlp/pallas_call | solution.py:783
  194.2 19.7 %middle.1 = (bf16[2048,768]{1,0:T(8,128)(2,1)}, f32[2048,768]{1,0:T(8,128)}, bf16[2048,768]{1,0:T(8,128)(2,1)}, bf16[768,768]{1,0:T(8,128)(2,1)}, f32[8,768]{1,0:T(8,128)}) custom-call(f32[2048,768]{1,0:T(8,128)} %get-tuple-element.51.resid_ref, f32[2048,768]{1,0:T(8,128)} %get-tuple-element.58.acc_ref, f32[2048,768]{1,0:T(8,128)} %get-tuple-element.59.dh_ref, ...), custom_call_target="tpu_custom_call" | custom-call | flops 4831838208 | bytes 37748736 | tf_op jit(solution)/shard_map/middle/pallas_call | solution.py:875
  214.0 77.6 %attend_back.1 = (bf16[3,2048,768]{2,1,0:T(8,128)(2,1)}, f32[48,768]{1,0:T(8,128)}, f32[48,3072]{1,0:T(8,128)}, f32[192,768]{1,0:T(8,128)}) custom-call(bf16[2048,2304]{1,0:T(8,128)(2,1)} %get-tuple-element.47.refs_0_.refs_1_.refs_2_, bf16[2048,2304]{1,0:T(8,128)(2,1)} %get-tuple-element.47.refs_0_.refs_1_.refs_2_, ...), custom_call_target="tpu_custom_call" | custom-call | flops 51539607552 | bytes 50331648 | tf_op jit(solution)/shard_map/attend_back/pallas_call | solution.py:678
  291.6 44.4 %finish.1 = (bf16[2048,768]{1,0:T(8,128)(2,1)}, f32[48,2304]{1,0:T(8,128)}, f32[16,128]{1,0:T(8,128)}) custom-call(bf16[768,2048]{1,0:T(8,128)(2,1)} %get-tuple-element.61.ht_ref, bf16[3,2048,768]{2,1,0:T(8,128)(2,1)} %get-tuple-element.68.part_ref.tile_ref, bf16[3,2048,768]{2,1,0:T(8,128)(2,1)} %get-tuple-element.68.part_ref.tile_ref, ...), custom_call_target="tpu_custom_call" | custom-call | flops 14495514624 | bytes 31457280 | tf_op jit(solution)/shard_map/finish/pallas_call | solution.py:1020
  336.0 0.0 copy-start.2
  336.0 0.7 slice_bitcast_fusion.1
  336.7 0.7 slice_bitcast_fusion.2
  337.4 1.5 slice_bitcast_fusion
  338.9 0.6 pad_maximum_fusion
  339.5 0.0 copy-start.3
  339.5 0.0 copy-start.1
  339.5 0.0 copy-start
  339.5 3.9 %copy.36 = bf16[2048,768]{1,0:T(8,128)(2,1)} copy(bf16[2048,768]{1,0:T(8,128)(2,1)} %get-tuple-element.103) | data formatting | bytes 6291456
  343.3 0.0 copy-done.2
  343.3 0.8 copy.37
  344.1 0.0 copy-done.3
  344.1 0.7 copy.38
  344.8 0.0 copy-done.1
  344.8 0.8 copy.39
  345.6 0.0 copy-done
  345.6 0.8 copy.40
Async XLA Ops:
  336.0 7.4 %copy-start.2 = (f32[48,2304]{1,0:T(8,128)S(1)}, f32[48,2304]{1,0:T(8,128)}, u32[]{:S(2)}) copy-start(f32[48,2304]{1,0:T(8,128)} %get-tuple-element.106) | copy-start | bytes 1327108
  339.5 4.6 %copy-start.3 = (f32[48,768]{1,0:T(8,128)S(1)}, f32[48,768]{1,0:T(8,128)}, u32[]{:S(2)}) copy-start(f32[48,768]{1,0:T(8,128)} %get-tuple-element.109) | copy-start | bytes 442372
  339.5 5.3 %copy-start.1 = (f32[48,3072]{1,0:T(8,128)S(1)}, f32[48,3072]{1,0:T(8,128)}, u32[]{:S(2)}) copy-start(f32[48,3072]{1,0:T(8,128)} %get-tuple-element.113) | copy-start | bytes 1769476
  339.5 6.1 %copy-start = (f32[192,768]{1,0:T(8,128)S(1)}, f32[192,768]{1,0:T(8,128)}, u32[]{:S(2)}) copy-start(f32[192,768]{1,0:T(8,128)} %get-tuple-element.115) | copy-start | bytes 1769476
where the time goes:
time: 347 us; the launch traced here: 346 us
  Pallas kernels  335 us (97%)
  local copies, waits for them, and re-layouts  9.84 us (3%)
    pallas_call x1, Pallas kernels, attend_back(): pl.pallas_call(functools.partial(attend_back_body, plan), grid=(mb, pairs...  77.6 us
    pallas_call x1, Pallas kernels, mlp(): pl.pallas_call(mlp_body, grid=(ff // FC,), in_specs=[whole, whole_t, whol...  72.3 us
    pallas_call x1, Pallas kernels, attend(): pl.pallas_call(functools.partial(attend_body, bool(shards)), grid=(mb, pa...  69.3 us
    pallas_call x1, Pallas kernels, finish(): pl.pallas_call(functools.partial(finish_body, plan), grid=(PHASES + tiles...  44.4 us
    pallas_call x1, Pallas kernels, first(): pl.pallas_call(first_body, in_specs=[vmem] * 9 + [ANY] * 3, out_specs=[AN...  42.1 us
    pallas_call x1, Pallas kernels, middle(): pl.pallas_call(mid_body, grid=(rows // tile,), in_specs=[blk, blk, blk, b...  19.7 us
    pallas_call x1, Pallas kernels, out_project(): pl.pallas_call(out_body, grid=(rows // tile,), in_specs=[blk, blk, pl.Blo...  9.9 us

commit v1 on v0

--- a/solution.py
+++ b/solution.py
@@ -505,9 +505,9 @@
 
 
 QT = 256
-GATHER_CUT = 6
-REDUCE_CUT = 3
-GATHER_LAGS = (0, 1, 3, 5, 7, 9)
+GATHER_CUT = (2, 8, 6)
+REDUCE_CUT = (1, 3, 3)
+GATHER_LAGS = (0, 1, 2, 4, 6, 8)
 REDUCE_LAGS = (0, 1, 4, 7, 10, 12, 12)
 
 
@@ -522,11 +522,8 @@
     return jnp.where(own, value, swap(value))
 
 
-def unit_list(widths, cut):
-    units = [(0, 0, widths[0])]
-    for i, w in enumerate(widths[1:]):
-        units += [(i + 1, j * (w // cut), w // cut) for j in range(cut)]
-    return units
+def unit_list(widths, cuts):
+    return [(i, j * (w // cut), w // cut) for i, (w, cut) in enumerate(zip(widths, cuts)) for j in range(cut)]
 
 
 def attend_body(hosting, *refs):
@@ -539,7 +536,7 @@
         hold = refs[15:18]
         units = [(shards[i], full[i], hold[i], col, n, True) for i, col, n in unit_list([s.shape[1] for s in shards], GATHER_CUT)]
         work = Gather(units, *refs[18:])
-        moves = [[2 + u + lag for lag in GATHER_LAGS] for u in range(len(units))]
+        moves = [[u + lag for lag in GATHER_LAGS] for u in range(len(units))]
     else:
         o_ref, p_ref, inv_ref, bias_ref, pair_ref = refs[4:]
     step = pl.program_id(0) * pl.num_programs(1) + pl.program_id(1)
@@ -557,7 +554,7 @@
     sums = []
     for hh in range(2):
         if hosting:
-            hooked(step, 2, hh, 12, moves, work, True)
+            hooked(step, 2, hh, 12, moves, work)
         own = lower if hh == 0 else ~lower
         q = q_ref[...].astype(F32) * LOG2E
         high = q.astype(BF16)
@@ -606,7 +603,7 @@
             *[whole(s) for s in shards],
         ],
         scratch_shapes=[pltpu.VMEM((ROWS, ROWS), F32), pltpu.VMEM((3, 2, ROWS, 128), BF16)]
-        + ([pltpu.VMEM(s.shape, s.dtype) for s in shards] + gather_sems(1 + 2 * GATHER_CUT) if shards else []),
+        + ([pltpu.VMEM(s.shape, s.dtype) for s in shards] + gather_sems(sum(GATHER_CUT)) if shards else []),
         compiler_params=params(**extra),
         name="attend",
         cost_estimate=pl.CostEstimate(
@@ -835,27 +832,33 @@
 
 
 def mid_body(resid_ref, acc_ref, dh_ref, g_ref, mixed_ref, w_ref, vec_ref,
-             y_ref, dr_ref, dm_ref, dw_ref, dvec_ref, sum_ref):
+             y_ref, dr_ref, dm_ref, dw_ref, dvec_ref, sum_ref, low_ref):
     step = pl.program_id(0)
-    resid = resid_ref[...]
-    y_ref[...] = (resid + acc_ref[...] + vec_ref[7:8, :]).astype(BF16)
-    g = g_ref[...].astype(F32)
-    n, inv = norm_stats(resid)
-    dh = dh_ref[...]
-    dr = g + norm_pull(dh, n, inv, vec_ref[5:6, :])
-    dr_ref[...] = dr
-    fold(dvec_ref, 4, step, dr)
-    fold(dvec_ref, 5, step, dh * n)
-    fold(dvec_ref, 6, step, dh)
-    fold(dvec_ref, 7, step, g)
-    low = dr.astype(BF16)
-    dm_ref[...] = mm(low, w_ref[...], NT).astype(BF16)
+
+    @pl.when(step == 0)
+    def _():
+        dvec_ref[...] = jnp.zeros_like(dvec_ref)
+
+    size = 128
+    for t in range(resid_ref.shape[0] // size):
+        sl = pl.ds(t * size, size)
+        resid = resid_ref[sl, :]
+        y_ref[sl, :] = (resid + acc_ref[sl, :] + vec_ref[7:8, :]).astype(BF16)
+        g = g_ref[sl, :].astype(F32)
+        n, inv = norm_stats(resid)
+        dh = dh_ref[sl, :]
+        dr = g + norm_pull(dh, n, inv, vec_ref[5:6, :])
+        dr_ref[sl, :] = dr
+        for row, value in ((4, dr), (5, dh * n), (6, dh), (7, g)):
+            dvec_ref[row : row + 1, :] += jnp.sum(value, axis=0, keepdims=True)
+        low_ref[sl, :] = dr.astype(BF16)
+        dm_ref[sl, :] = mm(low_ref[sl, :], w_ref[...], NT).astype(BF16)
+    low = low_ref[...]
     dw = mm(mixed_ref[...].T, low)
 
     @pl.when(step == 0)
     def _():
         sum_ref[...] = dw
-        dvec_ref[0:4, :] = jnp.zeros((4, dvec_ref.shape[1]), F32)
 
     @pl.when(step != 0)
     def _():
@@ -884,7 +887,7 @@
             jax.ShapeDtypeStruct((d, d), BF16),
             jax.ShapeDtypeStruct((8, d), F32),
         ],
-        scratch_shapes=[pltpu.VMEM((d, d), F32)],
+        scratch_shapes=[pltpu.VMEM((d, d), F32), pltpu.VMEM((tile, d), BF16)],
         compiler_params=params(),
         name="middle",
         cost_estimate=pl.CostEstimate(
@@ -1042,6 +1045,51 @@
     )(ht, dqkv, dqkv, x, dr, w, vec, dvec, dbu)
 
 
+def publish_body(splits, small_ref, *refs):
+    n = len(splits)
+    arrays, outs = refs[:n], refs[n : 2 * n]
+    vectors = refs[2 * n : 2 * n + 9]
+    holds = refs[2 * n + 9 : 3 * n + 9]
+    get_sem, put_sem = refs[3 * n + 9 :]
+    gets, puts = [], []
+    for src, out, hold, parts in zip(arrays, outs, holds, splits):
+        size = src.shape[0] // parts
+        for p in range(parts):
+            rows = pl.ds(p * size, size)
+            i = len(gets)
+            gets.append(pltpu.make_async_copy(src.at[rows], hold.at[rows], get_sem.at[i]))
+            puts.append(pltpu.make_async_copy(hold.at[rows], out.at[rows], put_sem.at[i]))
+    for get in gets:
+        get.start()
+    for i, ref in enumerate(vectors[:8]):
+        ref[...] = small_ref[i, 0 : ref.shape[0]]
+    up = vectors[8]
+    up[0:128] = small_ref[8, :]
+    up[128:] = small_ref[9, 0 : up.shape[0] - 128]
+    for get, put in zip(gets, puts):
+        get.wait()
+        put.start()
+    for put in puts:
+        put.wait()
+
+
+def publish(small, lengths, arrays):
+    splits = [8 if a.dtype == BF16 else 2 for a in arrays]
+    total = sum(splits)
+    vmem = pl.BlockSpec(memory_space=pltpu.VMEM)
+    return pl.pallas_call(
+        functools.partial(publish_body, splits),
+        in_specs=[vmem] + [ANY] * len(arrays),
+        out_specs=[ANY] * len(arrays) + [vmem] * 9,
+        out_shape=[jax.ShapeDtypeStruct(a.shape, a.dtype) for a in arrays]
+        + [jax.ShapeDtypeStruct((n,), F32) for n in lengths],
+        scratch_shapes=[pltpu.VMEM(a.shape, a.dtype) for a in arrays]
+        + [pltpu.SemaphoreType.DMA((total,)), pltpu.SemaphoreType.DMA((total,))],
+        compiler_params=params(),
+        name="publish",
+    )(small, *arrays)
+
+
 def on_device(tokens, cotangent, segment_ids, *shards):
     gather = lambda s: lax.all_gather(s, "fsdp", axis=0, tiled=True)
     n = lax.axis_size("fsdp")
@@ -1076,9 +1124,10 @@
     if near:
         dqkv, out_grad, up_grad, down_grad = attend_back(qkv, soft, mixed, dm, inv, (dwo, dwu, dwd))
         dx, triple_grad, small = finish(tokens, dr, first_t, dqkv, triple_weight, vec, dvec, dbu, True)
-        m = d // n
-        small_grads = [small[i, :m] for i in range(8)]
-        up_bias_grad = jnp.concatenate([small[8], small[9, : up_bias_s.shape[0] - 128]])
+        lengths = [d // n] * 8 + [up_bias_s.shape[0]]
+        dx, triple_grad, out_grad, up_grad, down_grad, *small_grads, up_bias_grad = publish(
+            small, lengths, (dx, triple_grad, out_grad, up_grad, down_grad)
+        )
     else:
         (dqkv,) = attend_back(qkv, soft, mixed, dm, inv)
         dx, dwt, dvec = finish(tokens, dr, first_t, dqkv, triple_weight, vec, dvec, dbu, False)

time: 347 us -> 339 us (0.977)
  local copies, waits for them, and re-layouts: 9.84 us -> 0 us
    unnamed x13 -> x0, local copies, waits for them, and re-layouts: 6.93 us -> none
    pallas_call x0 -> x1, Pallas kernels: none -> 5.81 us  [publish(): pl.pallas_call(functools.partial(publish_body, splits), in_specs=[vmem] +...]
where the time goes in v1:
time: 339 us; the launch traced here: 338 us
  Pallas kernels  337 us (99%)
    pallas_call x1, Pallas kernels, attend_back(): pl.pallas_call(functools.partial(attend_back_body, plan), grid=(mb, pairs...  77.8 us
    pallas_call x1, Pallas kernels, mlp(): pl.pallas_call(mlp_body, grid=(ff // FC,), in_specs=[whole, whole_t, whol...  72.2 us
    pallas_call x1, Pallas kernels, attend(): pl.pallas_call(functools.partial(attend_body, bool(shards)), grid=(mb, pa...  67.4 us
    pallas_call x1, Pallas kernels, finish(): pl.pallas_call(functools.partial(finish_body, plan), grid=(PHASES + tiles...  43 us
    pallas_call x1, Pallas kernels, first(): pl.pallas_call(first_body, in_specs=[vmem] * 9 + [ANY] * 3, out_specs=[AN...  42.2 us
    pallas_call x1, Pallas kernels, middle(): pl.pallas_call(mid_body, grid=(rows // tile,), in_specs=[blk, blk, blk, b...  18.9 us
    pallas_call x1, Pallas kernels, out_project(): pl.pallas_call(out_body, grid=(rows // tile,), in_specs=[blk, blk, pl.Blo...  9.72 us

profile of v1, /device:TPU:0, one launch (start us, length us, event | category | flops | bytes accessed | tf_op | source)
XLA Modules:
  0.0 338.0 jit_solution(17534829802198393046)
XLA Ops:
  0.6 42.2 %first.1 = (bf16[4,2,2,48,2304]{4,3,2,1,0:T(8,128)(2,1)}, f32[8,768]{1,0:T(8,128)}, f32[1,3072]{1,0:T(1,128)}, bf16[2048,2304]{1,0:T(8,128)(2,1)}, bf16[768,2048]{1,0:T(8,128)(2,1)}, /*index=5*/bf16[768,2048]{1,0:T(8,128)(2,1)}) custom-call(bf16[48]{0:T(256)(128)(2,1)} %refs_0_.1, bf16[48]{0:T(256)(128)(2,1)} %refs_1_.1, bf16[48]{0:T(256)(128)(2,1)} %refs_2_.1, ...), custom_call_target="tpu_custom_call" | custom-call | tf_op jit(solution)/shard_map/first/pallas_call | solution.py:432
  42.9 67.4 %attend.1 = (bf16[2048,768]{1,0:T(8,128)(2,1)}, bf16[2,12,1024,1024]{3,2,1,0:T(8,128)(2,1)}, f32[2048,768]{1,0:T(8,128)}, bf16[4,2,2,48,768]{4,3,2,1,0:T(8,128)(...) custom-call(bf16[2048,2304]{1,0:T(8,128)(2,1)} %get-tuple-element.61.refs_0_.refs_1_.refs_2_, ...), custom_call_target="tpu_custom_call" | custom-call | flops 25769803776 | bytes 50331648 | tf_op jit(solution)/shard_map/attend/pallas_call | solution.py:583
  110.3 9.7 %out_project.1 = (f32[2048,768]{1,0:T(8,128)}, bf16[2048,768]{1,0:T(8,128)(2,1)}, bf16[768,2048]{1,0:T(8,128)(2,1)}) custom-call(bf16[2048,768]{1,0:T(8,128)(2,1)} %x_ref.3, bf16[2048,768]{1,0:T(8,128)(2,1)} %get-tuple-element.62.m_ref.mixed_ref.refs_4_, bf16[768,768]{1,0:T(8,128)(2,1)} %bitcast.8, f32[8,768]{1,0:T(8,128)} %get-tuple-element.64.vec_ref), custom_call_target="tpu_custom_call" | custom-call | flops 2415919104 | bytes 18874368 | tf_op jit(solution)/shard_map/out_project/pallas_call | solution.py:717
  120.0 72.2 %mlp.1 = (f32[2048,768]{1,0:T(8,128)}, f32[2048,768]{1,0:T(8,128)}, bf16[768,3072]{1,0:T(8,128)(2,1)}, bf16[3072,768]{1,0:T(8,128)(2,1)}, f32[1,3072]{1,0:T(1,128)}) custom-call(bf16[2048,768]{1,0:T(8,128)(2,1)} %get-tuple-element.66.h_ref, bf16[768,2048]{1,0:T(8,128)(2,1)} %get-tuple-element.67.ht_ref, bf16[2048,768]{1,0:T(8,128)(2,1)} %g_ref.3, ...), custom_call_target="tpu_custom_call" | custom-call | flops 57982058496 | bytes 50331648 | tf_op jit(solution)/shard_map/mlp/pallas_call | solution.py:780
  192.2 18.9 %middle.1 = (bf16[2048,768]{1,0:T(8,128)(2,1)}, f32[2048,768]{1,0:T(8,128)}, bf16[2048,768]{1,0:T(8,128)(2,1)}, bf16[768,768]{1,0:T(8,128)(2,1)}, f32[8,768]{1,0:T(8,128)}) custom-call(f32[2048,768]{1,0:T(8,128)} %get-tuple-element.65.resid_ref, f32[2048,768]{1,0:T(8,128)} %get-tuple-element.72.acc_ref, f32[2048,768]{1,0:T(8,128)} %get-tuple-element.73.dh_ref, ...), custom_call_target="tpu_custom_call" | custom-call | flops 4831838208 | bytes 37748736 | tf_op jit(solution)/shard_map/middle/pallas_call | solution.py:878
  211.1 77.8 %attend_back.1 = (bf16[3,2048,768]{2,1,0:T(8,128)(2,1)}, f32[48,768]{1,0:T(8,128)}, f32[48,3072]{1,0:T(8,128)}, f32[192,768]{1,0:T(8,128)}) custom-call(bf16[2048,2304]{1,0:T(8,128)(2,1)} %get-tuple-element.61.refs_0_.refs_1_.refs_2_, bf16[2048,2304]{1,0:T(8,128)(2,1)} %get-tuple-element.61.refs_0_.refs_1_.refs_2_, ...), custom_call_target="tpu_custom_call" | custom-call | flops 51539607552 | bytes 50331648 | tf_op jit(solution)/shard_map/attend_back/pallas_call | solution.py:675
  288.9 43.0 %finish.1 = (bf16[2048,768]{1,0:T(8,128)(2,1)}, f32[48,2304]{1,0:T(8,128)}, f32[16,128]{1,0:T(8,128)}) custom-call(bf16[768,2048]{1,0:T(8,128)(2,1)} %get-tuple-element.75.ht_ref, bf16[3,2048,768]{2,1,0:T(8,128)(2,1)} %get-tuple-element.82.part_ref.tile_ref, bf16[3,2048,768]{2,1,0:T(8,128)(2,1)} %get-tuple-element.82.part_ref.tile_ref, ...), custom_call_target="tpu_custom_call" | custom-call | flops 14495514624 | bytes 31457280 | tf_op jit(solution)/shard_map/finish/pallas_call | solution.py:1023
  332.0 5.8 %publish.1 = (bf16[2048,768]{1,0:T(8,128)(2,1)}, f32[48,2304]{1,0:T(8,128)}, f32[48,768]{1,0:T(8,128)}, f32[48,3072]{1,0:T(8,128)}, f32[192,768]{1,0:T(8,128)}, ...) custom-call(f32[16,128]{1,0:T(8,128)} %get-tuple-element.87.small_re, ...), custom_call_target="tpu_custom_call" | custom-call | tf_op jit(solution)/shard_map/publish/pallas_call | solution.py:1080

commit v2 on v1

--- a/solution.py
+++ b/solution.py
@@ -371,19 +371,27 @@
     at_hook(0, moves, work)
     get_g.wait()
     for t in range(4):
-        part = slice(t * (rows // 4), (t + 1) * (rows // 4))
-        gt_ref[:, part] = g_ref[part, :].T
+
+        @pl.loop(0, rows // 4 // 128)
+        def _(i):
+            part = pl.ds(pl.multiple_of(t * (rows // 4) + i * 128, 128), 128)
+            gt_ref[:, part] = g_ref[part, :].T
+
         at_hook(1 + t, moves, work)
     put_g.start()
     get_x.wait()
     at_hook(5, moves, work)
     unpack(vec_ref, ub_ref, tall_ref)
     for t in range(4):
-        part = slice(t * (rows // 4), (t + 1) * (rows // 4))
-        n, _ = norm_stats(x_ref[part, :].astype(F32))
-        h = (n * vec_ref[0:1, :] + vec_ref[1:2, :]).astype(BF16)
-        h_ref[part, :] = h
-        ht_ref[:, part] = h.T
+
+        @pl.loop(0, rows // 4 // 128)
+        def _(i):
+            part = pl.ds(pl.multiple_of(t * (rows // 4) + i * 128, 128), 128)
+            n, _ = norm_stats(x_ref[part, :].astype(F32))
+            h = (n * vec_ref[0:1, :] + vec_ref[1:2, :]).astype(BF16)
+            h_ref[part, :] = h
+            ht_ref[:, part] = h.T
+
         at_hook(6 + t, moves, work)
     put_h.start()
 
@@ -753,20 +761,19 @@
 
     wu = wu_ref[...]
     wd = wd_ref[...]
-    dbu_ref[...] = jnp.zeros_like(dbu_ref)
-
-    @pl.loop(0, rows // RT)
-    def _(t):
-        sl = pl.ds(pl.multiple_of(t * RT, RT), RT)
+    bias_sum = None
+    for t in range(rows // RT):
+        sl = pl.ds(t * RT, RT)
         u = mm(h_ref[sl, :], wu) + bu_ref[...]
         act, slope = gelu_parts(u)
         act_ref[sl, :] = act.astype(BF16)
         du = mm(g_ref[sl, :], wd, NT) * slope
-        dbu_ref[...] += jnp.sum(du, axis=0, keepdims=True)
+        part = jnp.sum(du, axis=0, keepdims=True)
+        bias_sum = part if bias_sum is None else bias_sum + part
         du_ref[sl, :] = du.astype(BF16)
         acc_ref[sl, :] += mm(act_ref[sl, :], wd)
         dh_ref[sl, :] += mm(du_ref[sl, :], wu, NT)
-
+    dbu_ref[...] = bias_sum
     dwu_ref[...] = mm(ht_ref[...], du_ref[...]).astype(dwu_ref.dtype)
     dwd_ref[...] = mm(gt_ref[...], act_ref[...]).T.astype(dwd_ref.dtype)
 
@@ -840,6 +847,7 @@
         dvec_ref[...] = jnp.zeros_like(dvec_ref)
 
     size = 128
+
     for t in range(resid_ref.shape[0] // size):
         sl = pl.ds(t * size, size)
         resid = resid_ref[sl, :]

time: 339 us -> 337 us (level)
  no operation moved by 1% of the time
where the time goes in v2:
time: 337 us; the launch traced here: 336 us
  Pallas kernels  336 us (100%)
    pallas_call x1, Pallas kernels, attend_back(): pl.pallas_call(functools.partial(attend_back_body, plan), grid=(mb, pairs...  77.7 us
    pallas_call x1, Pallas kernels, mlp(): pl.pallas_call(mlp_body, grid=(ff // FC,), in_specs=[whole, whole_t, whol...  70.8 us
    pallas_call x1, Pallas kernels, attend(): pl.pallas_call(functools.partial(attend_body, bool(shards)), grid=(mb, pa...  67.4 us
    pallas_call x1, Pallas kernels, finish(): pl.pallas_call(functools.partial(finish_body, plan), grid=(PHASES + tiles...  43 us
    pallas_call x1, Pallas kernels, first(): pl.pallas_call(first_body, in_specs=[vmem] * 9 + [ANY] * 3, out_specs=[AN...  42.2 us
    pallas_call x1, Pallas kernels, middle(): pl.pallas_call(mid_body, grid=(rows // tile,), in_specs=[blk, blk, blk, b...  18.9 us
    pallas_call x1, Pallas kernels, out_project(): pl.pallas_call(out_body, grid=(rows // tile,), in_specs=[blk, blk, pl.Blo...  9.72 us

profile of v2, /device:TPU:0, one launch (start us, length us, event | category | flops | bytes accessed | tf_op | source)
XLA Modules:
  0.0 336.4 jit_solution(5388912851993798123)
XLA Ops:
  0.6 42.2 %first.1 = (bf16[4,2,2,48,2304]{4,3,2,1,0:T(8,128)(2,1)}, f32[8,768]{1,0:T(8,128)}, f32[1,3072]{1,0:T(1,128)}, bf16[2048,2304]{1,0:T(8,128)(2,1)}, bf16[768,2048]{1,0:T(8,128)(2,1)}, /*index=5*/bf16[768,2048]{1,0:T(8,128)(2,1)}) custom-call(bf16[48]{0:T(256)(128)(2,1)} %refs_0_.1, bf16[48]{0:T(256)(128)(2,1)} %refs_1_.1, bf16[48]{0:T(256)(128)(2,1)} %refs_2_.1, ...), custom_call_target="tpu_custom_call" | custom-call | tf_op jit(solution)/shard_map/first/pallas_call | solution.py:440
  42.9 67.4 %attend.1 = (bf16[2048,768]{1,0:T(8,128)(2,1)}, bf16[2,12,1024,1024]{3,2,1,0:T(8,128)(2,1)}, f32[2048,768]{1,0:T(8,128)}, bf16[4,2,2,48,768]{4,3,2,1,0:T(8,128)(...) custom-call(bf16[2048,2304]{1,0:T(8,128)(2,1)} %get-tuple-element.61.refs_0_.refs_1_.refs_2_, ...), custom_call_target="tpu_custom_call" | custom-call | flops 25769803776 | bytes 50331648 | tf_op jit(solution)/shard_map/attend/pallas_call | solution.py:591
  110.3 9.7 %out_project.1 = (f32[2048,768]{1,0:T(8,128)}, bf16[2048,768]{1,0:T(8,128)(2,1)}, bf16[768,2048]{1,0:T(8,128)(2,1)}) custom-call(bf16[2048,768]{1,0:T(8,128)(2,1)} %x_ref.3, bf16[2048,768]{1,0:T(8,128)(2,1)} %get-tuple-element.62.m_ref.mixed_ref.refs_4_, bf16[768,768]{1,0:T(8,128)(2,1)} %bitcast.8, f32[8,768]{1,0:T(8,128)} %get-tuple-element.64.vec_ref), custom_call_target="tpu_custom_call" | custom-call | flops 2415919104 | bytes 18874368 | tf_op jit(solution)/shard_map/out_project/pallas_call | solution.py:725
  120.0 70.8 %mlp.1 = (f32[2048,768]{1,0:T(8,128)}, f32[2048,768]{1,0:T(8,128)}, bf16[768,3072]{1,0:T(8,128)(2,1)}, bf16[3072,768]{1,0:T(8,128)(2,1)}, f32[1,3072]{1,0:T(1,128)}) custom-call(bf16[2048,768]{1,0:T(8,128)(2,1)} %get-tuple-element.66.h_ref, bf16[768,2048]{1,0:T(8,128)(2,1)} %get-tuple-element.67.ht_ref, bf16[2048,768]{1,0:T(8,128)(2,1)} %g_ref.3, ...), custom_call_target="tpu_custom_call" | custom-call | flops 57982058496 | bytes 50331648 | tf_op jit(solution)/shard_map/mlp/pallas_call | solution.py:787
  190.8 18.9 %middle.1 = (bf16[2048,768]{1,0:T(8,128)(2,1)}, f32[2048,768]{1,0:T(8,128)}, bf16[2048,768]{1,0:T(8,128)(2,1)}, bf16[768,768]{1,0:T(8,128)(2,1)}, f32[8,768]{1,0:T(8,128)}) custom-call(f32[2048,768]{1,0:T(8,128)} %get-tuple-element.65.resid_ref, f32[2048,768]{1,0:T(8,128)} %get-tuple-element.72.acc_ref, f32[2048,768]{1,0:T(8,128)} %get-tuple-element.73.dh_ref, ...), custom_call_target="tpu_custom_call" | custom-call | flops 4831838208 | bytes 37748736 | tf_op jit(solution)/shard_map/middle/pallas_call | solution.py:886
  209.7 77.7 %attend_back.1 = (bf16[3,2048,768]{2,1,0:T(8,128)(2,1)}, f32[48,768]{1,0:T(8,128)}, f32[48,3072]{1,0:T(8,128)}, f32[192,768]{1,0:T(8,128)}) custom-call(bf16[2048,2304]{1,0:T(8,128)(2,1)} %get-tuple-element.61.refs_0_.refs_1_.refs_2_, bf16[2048,2304]{1,0:T(8,128)(2,1)} %get-tuple-element.61.refs_0_.refs_1_.refs_2_, ...), custom_call_target="tpu_custom_call" | custom-call | flops 51539607552 | bytes 50331648 | tf_op jit(solution)/shard_map/attend_back/pallas_call | solution.py:683
  287.4 43.0 %finish.1 = (bf16[2048,768]{1,0:T(8,128)(2,1)}, f32[48,2304]{1,0:T(8,128)}, f32[16,128]{1,0:T(8,128)}) custom-call(bf16[768,2048]{1,0:T(8,128)(2,1)} %get-tuple-element.75.ht_ref, bf16[3,2048,768]{2,1,0:T(8,128)(2,1)} %get-tuple-element.82.part_ref.tile_ref, bf16[3,2048,768]{2,1,0:T(8,128)(2,1)} %get-tuple-element.82.part_ref.tile_ref, ...), custom_call_target="tpu_custom_call" | custom-call | flops 14495514624 | bytes 31457280 | tf_op jit(solution)/shard_map/finish/pallas_call | solution.py:1031
  330.4 5.8 %publish.1 = (bf16[2048,768]{1,0:T(8,128)(2,1)}, f32[48,2304]{1,0:T(8,128)}, f32[48,768]{1,0:T(8,128)}, f32[48,3072]{1,0:T(8,128)}, f32[192,768]{1,0:T(8,128)}, ...) custom-call(f32[16,128]{1,0:T(8,128)} %get-tuple-element.87.small_re, ...), custom_call_target="tpu_custom_call" | custom-call | tf_op jit(solution)/shard_map/publish/pallas_call | solution.py:1088

commit v3 on v2

--- a/solution.py
+++ b/solution.py
@@ -710,12 +710,15 @@
 
 
 def out_body(x_ref, m_ref, w_ref, vec_ref, resid_ref, h_ref, ht_ref):
-    resid = x_ref[...].astype(F32) + mm(m_ref[...], w_ref[...]) + vec_ref[4:5, :]
-    resid_ref[...] = resid
-    n, _ = norm_stats(resid)
-    h = (n * vec_ref[5:6, :] + vec_ref[6:7, :]).astype(BF16)
-    h_ref[...] = h
-    ht_ref[...] = h.T
+    size = 256
+    for t in range(x_ref.shape[0] // size):
+        sl = pl.ds(t * size, size)
+        resid = x_ref[sl, :].astype(F32) + mm(m_ref[sl, :], w_ref[...]) + vec_ref[4:5, :]
+        resid_ref[sl, :] = resid
+        n, _ = norm_stats(resid)
+        h = (n * vec_ref[5:6, :] + vec_ref[6:7, :]).astype(BF16)
+        h_ref[sl, :] = h
+        ht_ref[:, t * size : (t + 1) * size] = h.T
 
 
 def out_project(x, mixed, w, vec):
@@ -1082,7 +1085,7 @@
 
 
 def publish(small, lengths, arrays):
-    splits = [8 if a.dtype == BF16 else 2 for a in arrays]
+    splits = [2 if a.dtype == BF16 else 1 for a in arrays]
     total = sum(splits)
     vmem = pl.BlockSpec(memory_space=pltpu.VMEM)
     return pl.pallas_call(

time: 337 us -> 336 us (level)
  no operation moved by 1% of the time
where the time goes in v3:
time: 336 us
  Pallas kernels  335 us (100%)
    pallas_call x1, Pallas kernels, attend_back(): pl.pallas_call(functools.partial(attend_back_body, plan), grid=(mb, pairs...  77.9 us
    pallas_call x1, Pallas kernels, mlp(): pl.pallas_call(mlp_body, grid=(ff // FC,), in_specs=[whole, whole_t, whol...  70.7 us
    pallas_call x1, Pallas kernels, attend(): pl.pallas_call(functools.partial(attend_body, bool(shards)), grid=(mb, pa...  67.4 us
    pallas_call x1, Pallas kernels, finish(): pl.pallas_call(functools.partial(finish_body, plan), grid=(PHASES + tiles...  43.1 us
    pallas_call x1, Pallas kernels, first(): pl.pallas_call(first_body, in_specs=[vmem] * 9 + [ANY] * 3, out_specs=[AN...  42.2 us
    pallas_call x1, Pallas kernels, middle(): pl.pallas_call(mid_body, grid=(rows // tile,), in_specs=[blk, blk, blk, b...  18.9 us
    pallas_call x1, Pallas kernels, out_project(): pl.pallas_call(out_body, grid=(rows // tile,), in_specs=[blk, blk, pl.Blo...  9.62 us

profile of v3, /device:TPU:0, one launch (start us, length us, event | category | flops | bytes accessed | tf_op | source)
XLA Modules:
  0.0 335.7 jit_solution(14048678059075566599)
XLA Ops:
  0.6 42.2 %first.1 = (bf16[4,2,2,48,2304]{4,3,2,1,0:T(8,128)(2,1)}, f32[8,768]{1,0:T(8,128)}, f32[1,3072]{1,0:T(1,128)}, bf16[2048,2304]{1,0:T(8,128)(2,1)}, bf16[768,2048]{1,0:T(8,128)(2,1)}, /*index=5*/bf16[768,2048]{1,0:T(8,128)(2,1)}) custom-call(bf16[48]{0:T(256)(128)(2,1)} %refs_0_.1, bf16[48]{0:T(256)(128)(2,1)} %refs_1_.1, bf16[48]{0:T(256)(128)(2,1)} %refs_2_.1, ...), custom_call_target="tpu_custom_call" | custom-call | tf_op jit(solution)/shard_map/first/pallas_call | solution.py:440
  42.9 67.4 %attend.1 = (bf16[2048,768]{1,0:T(8,128)(2,1)}, bf16[2,12,1024,1024]{3,2,1,0:T(8,128)(2,1)}, f32[2048,768]{1,0:T(8,128)}, bf16[4,2,2,48,768]{4,3,2,1,0:T(8,128)(...) custom-call(bf16[2048,2304]{1,0:T(8,128)(2,1)} %get-tuple-element.61.refs_0_.refs_1_.refs_2_, ...), custom_call_target="tpu_custom_call" | custom-call | flops 25769803776 | bytes 50331648 | tf_op jit(solution)/shard_map/attend/pallas_call | solution.py:591
  110.3 9.6 %out_project.1 = (f32[2048,768]{1,0:T(8,128)}, bf16[2048,768]{1,0:T(8,128)(2,1)}, bf16[768,2048]{1,0:T(8,128)(2,1)}) custom-call(bf16[2048,768]{1,0:T(8,128)(2,1)} %x_ref.3, bf16[2048,768]{1,0:T(8,128)(2,1)} %get-tuple-element.62.m_ref.mixed_ref.refs_4_, bf16[768,768]{1,0:T(8,128)(2,1)} %bitcast.8, f32[8,768]{1,0:T(8,128)} %get-tuple-element.64.vec_ref), custom_call_target="tpu_custom_call" | custom-call | flops 2415919104 | bytes 18874368 | tf_op jit(solution)/shard_map/out_project/pallas_call | solution.py:728
  119.9 70.7 %mlp.1 = (f32[2048,768]{1,0:T(8,128)}, f32[2048,768]{1,0:T(8,128)}, bf16[768,3072]{1,0:T(8,128)(2,1)}, bf16[3072,768]{1,0:T(8,128)(2,1)}, f32[1,3072]{1,0:T(1,128)}) custom-call(bf16[2048,768]{1,0:T(8,128)(2,1)} %get-tuple-element.66.h_ref, bf16[768,2048]{1,0:T(8,128)(2,1)} %get-tuple-element.67.ht_ref, bf16[2048,768]{1,0:T(8,128)(2,1)} %g_ref.3, ...), custom_call_target="tpu_custom_call" | custom-call | flops 57982058496 | bytes 50331648 | tf_op jit(solution)/shard_map/mlp/pallas_call | solution.py:790
  190.6 18.9 %middle.1 = (bf16[2048,768]{1,0:T(8,128)(2,1)}, f32[2048,768]{1,0:T(8,128)}, bf16[2048,768]{1,0:T(8,128)(2,1)}, bf16[768,768]{1,0:T(8,128)(2,1)}, f32[8,768]{1,0:T(8,128)}) custom-call(f32[2048,768]{1,0:T(8,128)} %get-tuple-element.65.resid_ref, f32[2048,768]{1,0:T(8,128)} %get-tuple-element.72.acc_ref, f32[2048,768]{1,0:T(8,128)} %get-tuple-element.73.dh_ref, ...), custom_call_target="tpu_custom_call" | custom-call | flops 4831838208 | bytes 37748736 | tf_op jit(solution)/shard_map/middle/pallas_call | solution.py:889
  209.4 77.9 %attend_back.1 = (bf16[3,2048,768]{2,1,0:T(8,128)(2,1)}, f32[48,768]{1,0:T(8,128)}, f32[48,3072]{1,0:T(8,128)}, f32[192,768]{1,0:T(8,128)}) custom-call(bf16[2048,2304]{1,0:T(8,128)(2,1)} %get-tuple-element.61.refs_0_.refs_1_.refs_2_, bf16[2048,2304]{1,0:T(8,128)(2,1)} %get-tuple-element.61.refs_0_.refs_1_.refs_2_, ...), custom_call_target="tpu_custom_call" | custom-call | flops 51539607552 | bytes 50331648 | tf_op jit(solution)/shard_map/attend_back/pallas_call | solution.py:683
  287.4 43.1 %finish.1 = (bf16[2048,768]{1,0:T(8,128)(2,1)}, f32[48,2304]{1,0:T(8,128)}, f32[16,128]{1,0:T(8,128)}) custom-call(bf16[768,2048]{1,0:T(8,128)(2,1)} %get-tuple-element.75.ht_ref, bf16[3,2048,768]{2,1,0:T(8,128)(2,1)} %get-tuple-element.82.part_ref.tile_ref, bf16[3,2048,768]{2,1,0:T(8,128)(2,1)} %get-tuple-element.82.part_ref.tile_ref, ...), custom_call_target="tpu_custom_call" | custom-call | flops 14495514624 | bytes 31457280 | tf_op jit(solution)/shard_map/finish/pallas_call | solution.py:1034
  330.5 5.1 %publish.1 = (bf16[2048,768]{1,0:T(8,128)(2,1)}, f32[48,2304]{1,0:T(8,128)}, f32[48,768]{1,0:T(8,128)}, f32[48,3072]{1,0:T(8,128)}, f32[192,768]{1,0:T(8,128)}, ...) custom-call(f32[16,128]{1,0:T(8,128)} %get-tuple-element.87.small_re, ...), custom_call_target="tpu_custom_call" | custom-call | tf_op jit(solution)/shard_map/publish/pallas_call | solution.py:1091

commit v4 on v3

--- a/solution.py
+++ b/solution.py
@@ -513,6 +513,7 @@
 
 
 QT = 256
+BACK_TILE = 512
 GATHER_CUT = (2, 8, 6)
 REDUCE_CUT = (1, 3, 3)
 GATHER_LAGS = (0, 1, 2, 4, 6, 8)
@@ -652,9 +653,9 @@
         pair = jnp.where(own, high, swap(low))
         center = jnp.sum(jnp.where(own, g * o_ref[...].astype(F32), 0.0), axis=-1, keepdims=True)
         v = twice(v_ref[...], own)
-        for t in range(rows // QT):
-            sl = pl.ds(t * QT, QT)
-            ts = slice(t * QT, (t + 1) * QT)
+        for t in range(rows // BACK_TILE):
+            sl = pl.ds(t * BACK_TILE, BACK_TILE)
+            ts = slice(t * BACK_TILE, (t + 1) * BACK_TILE)
             d_soft = mm(pair[ts, :], v, NT)
             ds_ref[hh, sl, :] = (p_ref[hh, sl, :].astype(F32) * (d_soft - center[ts, :])).astype(BF16)
         dv = mm(pair.T, p_ref[hh])

time: 336 us -> 337 us (level)
  no operation moved by 1% of the time
where the time goes in v4:
time: 337 us; the launch traced here: 336 us
  Pallas kernels  335 us (99%)
    pallas_call x1, Pallas kernels, attend_back(): pl.pallas_call(functools.partial(attend_back_body, plan), grid=(mb, pairs...  77.6 us
    pallas_call x1, Pallas kernels, mlp(): pl.pallas_call(mlp_body, grid=(ff // FC,), in_specs=[whole, whole_t, whol...  70.7 us
    pallas_call x1, Pallas kernels, attend(): pl.pallas_call(functools.partial(attend_body, bool(shards)), grid=(mb, pa...  67.4 us
    pallas_call x1, Pallas kernels, finish(): pl.pallas_call(functools.partial(finish_body, plan), grid=(PHASES + tiles...  43.7 us
    pallas_call x1, Pallas kernels, first(): pl.pallas_call(first_body, in_specs=[vmem] * 9 + [ANY] * 3, out_specs=[AN...  42.2 us
    pallas_call x1, Pallas kernels, middle(): pl.pallas_call(mid_body, grid=(rows // tile,), in_specs=[blk, blk, blk, b...  18.9 us
    pallas_call x1, Pallas kernels, out_project(): pl.pallas_call(out_body, grid=(rows // tile,), in_specs=[blk, blk, pl.Blo...  9.62 us

profile of v4, /device:TPU:0, one launch (start us, length us, event | category | flops | bytes accessed | tf_op | source)
XLA Modules:
  0.0 336.0 jit_solution(851448457812288029)
XLA Ops:
  0.6 42.2 %first.1 = (bf16[4,2,2,48,2304]{4,3,2,1,0:T(8,128)(2,1)}, f32[8,768]{1,0:T(8,128)}, f32[1,3072]{1,0:T(1,128)}, bf16[2048,2304]{1,0:T(8,128)(2,1)}, bf16[768,2048]{1,0:T(8,128)(2,1)}, /*index=5*/bf16[768,2048]{1,0:T(8,128)(2,1)}) custom-call(bf16[48]{0:T(256)(128)(2,1)} %refs_0_.1, bf16[48]{0:T(256)(128)(2,1)} %refs_1_.1, bf16[48]{0:T(256)(128)(2,1)} %refs_2_.1, ...), custom_call_target="tpu_custom_call" | custom-call | tf_op jit(solution)/shard_map/first/pallas_call | solution.py:440
  42.9 67.4 %attend.1 = (bf16[2048,768]{1,0:T(8,128)(2,1)}, bf16[2,12,1024,1024]{3,2,1,0:T(8,128)(2,1)}, f32[2048,768]{1,0:T(8,128)}, bf16[4,2,2,48,768]{4,3,2,1,0:T(8,128)(...) custom-call(bf16[2048,2304]{1,0:T(8,128)(2,1)} %get-tuple-element.61.refs_0_.refs_1_.refs_2_, ...), custom_call_target="tpu_custom_call" | custom-call | flops 25769803776 | bytes 50331648 | tf_op jit(solution)/shard_map/attend/pallas_call | solution.py:592
  110.3 9.6 %out_project.1 = (f32[2048,768]{1,0:T(8,128)}, bf16[2048,768]{1,0:T(8,128)(2,1)}, bf16[768,2048]{1,0:T(8,128)(2,1)}) custom-call(bf16[2048,768]{1,0:T(8,128)(2,1)} %x_ref.3, bf16[2048,768]{1,0:T(8,128)(2,1)} %get-tuple-element.62.m_ref.mixed_ref.refs_4_, bf16[768,768]{1,0:T(8,128)(2,1)} %bitcast.8, f32[8,768]{1,0:T(8,128)} %get-tuple-element.64.vec_ref), custom_call_target="tpu_custom_call" | custom-call | flops 2415919104 | bytes 18874368 | tf_op jit(solution)/shard_map/out_project/pallas_call | solution.py:729
  119.9 70.7 %mlp.1 = (f32[2048,768]{1,0:T(8,128)}, f32[2048,768]{1,0:T(8,128)}, bf16[768,3072]{1,0:T(8,128)(2,1)}, bf16[3072,768]{1,0:T(8,128)(2,1)}, f32[1,3072]{1,0:T(1,128)}) custom-call(bf16[2048,768]{1,0:T(8,128)(2,1)} %get-tuple-element.66.h_ref, bf16[768,2048]{1,0:T(8,128)(2,1)} %get-tuple-element.67.ht_ref, bf16[2048,768]{1,0:T(8,128)(2,1)} %g_ref.3, ...), custom_call_target="tpu_custom_call" | custom-call | flops 57982058496 | bytes 50331648 | tf_op jit(solution)/shard_map/mlp/pallas_call | solution.py:791
  190.6 18.9 %middle.1 = (bf16[2048,768]{1,0:T(8,128)(2,1)}, f32[2048,768]{1,0:T(8,128)}, bf16[2048,768]{1,0:T(8,128)(2,1)}, bf16[768,768]{1,0:T(8,128)(2,1)}, f32[8,768]{1,0:T(8,128)}) custom-call(f32[2048,768]{1,0:T(8,128)} %get-tuple-element.65.resid_ref, f32[2048,768]{1,0:T(8,128)} %get-tuple-element.72.acc_ref, f32[2048,768]{1,0:T(8,128)} %get-tuple-element.73.dh_ref, ...), custom_call_target="tpu_custom_call" | custom-call | flops 4831838208 | bytes 37748736 | tf_op jit(solution)/shard_map/middle/pallas_call | solution.py:890
  209.4 77.6 %attend_back.1 = (bf16[3,2048,768]{2,1,0:T(8,128)(2,1)}, f32[48,768]{1,0:T(8,128)}, f32[48,3072]{1,0:T(8,128)}, f32[192,768]{1,0:T(8,128)}) custom-call(bf16[2048,2304]{1,0:T(8,128)(2,1)} %get-tuple-element.61.refs_0_.refs_1_.refs_2_, bf16[2048,2304]{1,0:T(8,128)(2,1)} %get-tuple-element.61.refs_0_.refs_1_.refs_2_, ...), custom_call_target="tpu_custom_call" | custom-call | flops 51539607552 | bytes 50331648 | tf_op jit(solution)/shard_map/attend_back/pallas_call | solution.py:684
  287.1 43.7 %finish.1 = (bf16[2048,768]{1,0:T(8,128)(2,1)}, f32[48,2304]{1,0:T(8,128)}, f32[16,128]{1,0:T(8,128)}) custom-call(bf16[768,2048]{1,0:T(8,128)(2,1)} %get-tuple-element.75.ht_ref, bf16[3,2048,768]{2,1,0:T(8,128)(2,1)} %get-tuple-element.82.part_ref.tile_ref, bf16[3,2048,768]{2,1,0:T(8,128)(2,1)} %get-tuple-element.82.part_ref.tile_ref, ...), custom_call_target="tpu_custom_call" | custom-call | flops 14495514624 | bytes 31457280 | tf_op jit(solution)/shard_map/finish/pallas_call | solution.py:1035
  330.8 5.1 %publish.1 = (bf16[2048,768]{1,0:T(8,128)(2,1)}, f32[48,2304]{1,0:T(8,128)}, f32[48,768]{1,0:T(8,128)}, f32[48,3072]{1,0:T(8,128)}, f32[192,768]{1,0:T(8,128)}, ...) custom-call(f32[16,128]{1,0:T(8,128)} %get-tuple-element.87.small_re, ...), custom_call_target="tpu_custom_call" | custom-call | tf_op jit(solution)/shard_map/publish/pallas_call | solution.py:1092
